TPU v7x, 512 devices: a whole 4x4x16 slice. The times are simulated.
512 devices in a mesh: pre: 16 (over z), row: 32 (over x, y, core).
Axes of the slice: x: 4, y: 4, z: 16, core: 2. Of those that a mesh axis runs over, the one named last changes fastest.
Arguments:
- hidden_in: bfloat16 [4096, 8192], P('row'), may hold values from -6 to 6
- frozen_query_base: bfloat16 [4096, 1024], P('row'), may hold values from -10 to 10
- k_prefix: bfloat16 [32768, 128], P('pre'), may hold values from -6 to 6
- v_prefix: bfloat16 [32768, 128], P('pre'), may hold values from -6 to 6
- tree_mask: int32 [8, 256], P(None, 'pre'), may hold values from 0 to 1, as said below
- adapter_ids: int32 [8], replicated, may hold values from 0 to 7, each once
- a_down: bfloat16 [8192, 128], P('row'), may hold values from -0.0625 to 0.0625
- up_weight_matrix: bfloat16 [128, 1024], replicated, may hold values from -0.75 to 0.75
- cotangent: bfloat16 [4096, 1024], P('row'), may hold values from -6 to 6
Outputs:
- attended: bfloat16 [4096, 1024], P('row')
- grad_a: float32 [8192, 128], P('row')
- up_weight_gradient: float32 [128, 1024], replicated
Inputs may be any that keep to these rules, and one draw needn't show every extreme that they name: `tree_mask`: every student reads mask block 0. The blocks that a student reads lie on one path of a tree of branches shared by the students: blocks near the start of the prefix are read by more students than blocks near its end.
All inputs are finite; a program needn't handle non-finite values.
Results may differ from a plain program's by a relative error of at most 0.014.
Values may be sent and summed in bfloat16 or wider, within the bound.
A program may use at most 64 MiB of HBM per device.

v0:
```python
import math

import jax
import jax.numpy as jnp
from jax import lax
from jax.sharding import PartitionSpec as P

HD = 128
RANK = 16
S = 8
CONT = 512
MB = 128
BLOCK = 1024


ADAPTER_SCALE = 2.0
VERY_LOW = -1e30


def combined_all(part, axis, combine):
    gathered = jax.tree.map(lambda a: lax.all_gather(a, axis), part)

    def take(source):
        return jax.tree.map(lambda a: lax.dynamic_index_in_dim(a, source, 0, False), gathered)

    return lax.fori_loop(
        1, lax.axis_size(axis), lambda source, state: combine(state, take(source)), take(0)
    )


def combine_partials(first, second):
    first_max, first_sum, first_out = first
    second_max, second_sum, second_out = second
    new_max = jnp.maximum(first_max, second_max)
    first_factor = jnp.exp(first_max - new_max)
    second_factor = jnp.exp(second_max - new_max)
    new_sum = first_sum * first_factor + second_sum * second_factor
    new_out = first_out * first_factor[:, None] + second_out * second_factor[:, None]
    return (new_max, new_sum, new_out)


def shards(
    hidden_in,
    frozen_query_base,
    k_prefix,
    v_prefix,
    tree_mask,
    adapter_ids,
    a_down,
    up_weight_matrix,
    cotangent,
):
    token_count = hidden_in.shape[0]
    head_count = frozen_query_base.shape[1] // HD
    rank_cols = a_down.shape[1]
    score_scale = 1.0 / math.sqrt(HD)
    row_index = lax.axis_index("row")
    student = row_index * token_count // CONT
    chosen = jnp.arange(S) == student
    adapter = jnp.sum(jnp.where(chosen, adapter_ids, 0))
    live_blocks = jnp.sum(jnp.where(chosen[:, None], tree_mask, 0), axis=0)
    column_mask = jnp.arange(rank_cols) // RANK == adapter
    columns = hidden_in
    latent_full = jnp.dot(
        columns,
        lax.all_gather(a_down, "row", axis=0, tiled=True),
        preferred_element_type=jnp.float32,
    )
    low_rank_code = jnp.where(column_mask[None, :], latent_full, 0.0).astype(jnp.bfloat16)
    raised_query = jnp.dot(low_rank_code, up_weight_matrix, preferred_element_type=jnp.float32)
    student_queries = (frozen_query_base.astype(jnp.float32) + ADAPTER_SCALE * raised_query).astype(
        jnp.bfloat16
    )
    row_count = token_count * head_count
    query_rows = student_queries.reshape(row_count, HD)
    upstream = cotangent.reshape(row_count, HD)
    block_count = k_prefix.shape[0] // BLOCK
    per_block = BLOCK // MB

    def block_flags(block_index):
        return lax.dynamic_slice_in_dim(live_blocks, block_index * per_block, per_block, 0) > 0

    def block_scores(block_index):
        key_block = lax.dynamic_slice_in_dim(k_prefix, block_index * BLOCK, BLOCK, 0)
        value_block = lax.dynamic_slice_in_dim(v_prefix, block_index * BLOCK, BLOCK, 0)
        live_flags = block_flags(block_index)
        live_keys = jnp.broadcast_to(live_flags[:, None], (per_block, MB)).reshape(BLOCK)
        scores = (
            lax.dot_general(
                query_rows, key_block, (((1,), (1,)), ((), ())), preferred_element_type=jnp.float32
            )
            * score_scale
        )
        return (key_block, value_block, live_keys, scores)

    def forward_block(block_index, carried):
        running_max, running_sum, running_out = carried
        key_block, value_block, live_keys, scores = block_scores(block_index)
        masked = jnp.where(live_keys[None, :], scores, VERY_LOW)
        new_max = jnp.maximum(running_max, jnp.max(masked, axis=1))
        weights = jnp.where(live_keys[None, :], jnp.exp(scores - new_max[:, None]), 0.0)
        factor = jnp.exp(running_max - new_max)
        new_sum = running_sum * factor + jnp.sum(weights, axis=1)
        new_out = running_out * factor[:, None] + jnp.dot(
            weights.astype(jnp.bfloat16), value_block, preferred_element_type=jnp.float32
        )
        return (new_max, new_sum, new_out)

    def forward_step(block_index, carried):
        return forward_block(block_index, carried)

    start_state = (
        jnp.full((row_count,), VERY_LOW, jnp.float32),
        jnp.zeros((row_count,), jnp.float32),
        jnp.zeros((row_count, HD), jnp.float32),
    )
    local_max, local_sum, local_out = lax.fori_loop(0, block_count, forward_step, start_state)
    row_max, row_total, merged_out = combined_all(
        (local_max, local_sum, local_out), "pre", combine_partials
    )
    attended_rows = (merged_out / row_total[:, None]).astype(jnp.bfloat16)
    log_total = row_max + jnp.log(row_total)
    row_delta = jnp.sum(upstream.astype(jnp.float32) * attended_rows.astype(jnp.float32), axis=1)

    def backward_block(block_index, accum):
        key_block, value_block, live_keys, scores = block_scores(block_index)
        prob_block = jnp.where(live_keys[None, :], jnp.exp(scores - log_total[:, None]), 0.0)
        grad_probs = lax.dot_general(
            upstream, value_block, (((1,), (1,)), ((), ())), preferred_element_type=jnp.float32
        )
        grad_scores = (prob_block * (grad_probs - row_delta[:, None])).astype(jnp.bfloat16)
        return accum + jnp.dot(grad_scores, key_block, preferred_element_type=jnp.float32)

    def backward_step(block_index, accum):
        return backward_block(block_index, accum)

    partial_grad = lax.fori_loop(
        0, block_count, backward_step, jnp.zeros((row_count, HD), jnp.float32)
    )
    summed_grad = lax.psum(partial_grad, "pre") * score_scale
    query_gradient = summed_grad.reshape(token_count, head_count * HD).astype(jnp.bfloat16)
    backward_low_rank = ADAPTER_SCALE * lax.dot_general(
        query_gradient,
        up_weight_matrix,
        (((1,), (1,)), ((), ())),
        preferred_element_type=jnp.float32,
    )
    grad_latent = jnp.where(column_mask[None, :], backward_low_rank, 0.0).astype(jnp.bfloat16)
    partial_up_weight = ADAPTER_SCALE * lax.dot_general(
        low_rank_code, query_gradient, (((0,), (0,)), ((), ())), preferred_element_type=jnp.float32
    )
    up_weight_gradient = lax.psum(partial_up_weight, "row")
    columns = hidden_in
    grad_a = lax.psum_scatter(
        lax.dot_general(
            columns, grad_latent, (((0,), (0,)), ((), ())), preferred_element_type=jnp.float32
        ),
        "row",
        scatter_dimension=0,
        tiled=True,
    )
    attended = attended_rows.reshape(token_count, head_count * HD)
    return (attended, grad_a, up_weight_gradient)


def solution(mesh):
    in_specs = (
        P("row", None),
        P("row", None),
        P("pre", None),
        P("pre", None),
        P(None, "pre"),
        P(),
        P("row", None),
        P(),
        P("row", None),
    )
    out_specs = (P("row", None), P("row", None), P())
    return jax.shard_map(shards, mesh=mesh, in_specs=in_specs, out_specs=out_specs, check_vma=False)
```

profile of v0, /device:TPU:1, one launch (start us, length us, event | category | flops | bytes accessed | tf_op | source)
XLA Modules:
  0.0 645.0 jit_solution(6842407134143778521)
XLA Ops:
  8.1 1.4 select_reduce_fusion.2
  10.1 0.8 select_reduce_fusion.1
  10.8 64.9 %all-gather.6.cloned.1.call-done = bf16[8192,128]{1,0:T(8,128)(2,1)} async-done(((bf16[256,128]{1,0:T(8,128)(2,1)}), bf16[8192,128]{1,0:T(8,128)(2,1)}) %all-gather.6.cloned.1.call-update) | async-done | bytes 2097168 | tf_op jit(solution)/shard_map/all_gather | solution.py:66
  75.8 2.3 fusion.33
  78.4 18.8 %while.52 = (s32[]{:T(128)}, f32[1024]{0:T(1024)S(1)}, f32[1024]{0:T(1024)S(1)}, f32[1024,128]{1,0:T(8,128)}, s32[16]{0:T(128)S(1)}, /*index=5*/bf16[2048,128]{1...) while((s32[]{:T(128)}, f32[1024]{0:T(1024)S(1)}, ...), condition=%wide.region_5.6_spmd.clone, body=%wide.region_2.5_spmd.clone.sunk | while | flops 548803584 | bytes 35459452 | solution.py:117
  78.6 2.7 select_reduce_fusion.4
  81.3 3.2 fusion.70
  84.7 2.3 fusion.72
  88.0 2.7 select_reduce_fusion.4
  90.7 3.2 fusion.70
  94.1 2.3 fusion.72
  97.3 1.8 reshape.55
  99.1 25.1 %all-gather = f32[16384]{0:T(1024)S(1)} all-gather(f32[1024]{0:T(1024)S(1)} %get-tuple-element.476), channel_id=2, replica_groups=mesh['pre'=16,'row'=32] {'pre'}, dimensions={0}, use_global_device_ids=true | all-gather | bytes 69632 | tf_op jit(solution)/shard_map/all_gather | solution.py:21
  124.2 24.6 %all-gather.1 = f32[16384]{0:T(1024)S(1)} all-gather(f32[1024]{0:T(1024)S(1)} %get-tuple-element.477), channel_id=3, replica_groups=mesh['pre'=16,'row'=32] {'pre'}, dimensions={0}, use_global_device_ids=true | all-gather | bytes 69632 | tf_op jit(solution)/shard_map/all_gather | solution.py:21
  149.4 53.7 %all-gather.8.cloned.1.call-done = f32[16384,128]{1,0:T(8,128)} async-done(((f32[1024,128]{1,0:T(8,128)}), f32[16384,128]{1,0:T(8,128)}) %all-gather.8.cloned.1.call-update) | async-done | bytes 8388624 | tf_op jit(solution)/shard_map/all_gather | solution.py:21
  203.2 1.1 slice.8
  204.2 34.6 %while.51 = (s32[]{:T(128)}, f32[1024]{0:T(1024)S(1)}, f32[1024]{0:T(1024)S(1)}, f32[1024,128]{1,0:T(8,128)S(1)}, f32[16,1024]{1,0:T(8,128)S(1)}, /*index=5*/f32...) while((s32[]{:T(128)}, f32[1024]{0:T(1024)S(1)}, f32[1024]{0:T(1024)S(1)}, ...), condition=%wide.region_7.8_spmd, body=%wide.region_6.7_spmd.sunk | while | flops 399365 | bytes 1630359 | solution.py:26
  204.2 0.8 constant_dynamic-slice_fusion.3
  205.0 1.5 fusion.66
  207.3 1.5 fusion.66
  209.6 1.5 fusion.66
  212.0 1.5 fusion.66
  214.3 1.5 fusion.66
  216.6 1.5 fusion.66
  218.9 1.5 fusion.66
  221.2 1.5 fusion.66
  223.5 1.5 fusion.66
  225.8 1.5 fusion.66
  228.1 1.5 fusion.66
  230.4 1.5 fusion.66
  232.7 1.5 fusion.66
  235.0 1.5 fusion.66
  237.3 1.5 fusion.66
  238.9 1.9 multiply_reduce_fusion
  240.7 15.4 %while.53 = (s32[]{:T(128)}, f32[1024,128]{1,0:T(8,128)}, s32[16]{0:T(128)S(1)}, bf16[2048,128]{1,0:T(8,128)(2,1)S(1)}, bf16[1024,128]{1,0:T(8,128)(2,1)S(1)}, /...) while((s32[]{:T(128)}, f32[1024,128]{1,0:T(8,128)}, ...), condition=%wide.region_10.11_spmd.clone, body=%wide.region_9.10_spmd.clone.sunk | while | flops 811859968 | bytes 11808582 | solution.py:137
  240.7 2.7 fusion.78
  243.5 4.8 fusion.79
  248.4 2.7 fusion.78
  251.2 4.9 fusion.79
  256.2 126.1 %all-reduce.3.cloned.1.call-done = f32[1024,128]{1,0:T(8,128)} async-done(((f32[1024,128]{1,0:T(8,128)}), f32[1024,128]{1,0:T(8,128)}) %all-reduce.3.cloned.1.call-update) | async-done | bytes 524304 | tf_op jit(solution)/shard_map/psum | solution.py:140
  382.3 1.1 multiply_convert_fusion.1
  383.5 3.0 convolution_bitcast_fusion
  386.6 1.1 convolution_multiply_fusion
  387.7 0.8 reshape.54
  388.5 108.3 %reduce-scatter.2.cloned.1.call-done = f32[256,128]{0,1:T(8,128)} async-done(((f32[8192,128]{0,1:T(8,128)}), f32[256,128]{0,1:T(8,128)}) %reduce-scatter.2.cloned.1.call-update) | async-done | bytes 131088 | tf_op jit(solution)/shard_map/reduce_scatter | solution.py:154
  496.8 1.7 copy.13
  498.4 138.2 %all-reduce.5.cloned.1.call-done = f32[128,1024]{1,0:T(8,128)} async-done(((f32[128,1024]{1,0:T(8,128)}), f32[128,1024]{1,0:T(8,128)}) %all-reduce.5.cloned.1.call-update) | async-done | bytes 524304 | tf_op jit(solution)/shard_map/psum | solution.py:152
  636.6 1.9 copy.46
  (95 shorter events, 16.4 us)
Async XLA Ops:
  7.2 68.6 %copy-start = (bf16[128,8192]{1,0:T(8,128)(2,1)S(1)}, bf16[128,8192]{1,0:T(8,128)(2,1)}, u32[]{:S(2)}) copy-start(bf16[128,8192]{1,0:T(8,128)(2,1)} %param.15) | copy-start | bytes 6291460
  7.2 70.9 %copy-start.9 = (bf16[128,1024]{1,0:T(8,128)(2,1)S(1)}, bf16[128,1024]{1,0:T(8,128)(2,1)}, u32[]{:S(2)}) copy-start(bf16[128,1024]{1,0:T(8,128)(2,1)} %param.16) | copy-start | bytes 786436
  7.2 70.9 %copy-start.3 = (bf16[128,1024]{1,0:T(8,128)(2,1)S(1)}, bf16[128,1024]{1,0:T(8,128)(2,1)}, u32[]{:S(2)}) copy-start(bf16[128,1024]{1,0:T(8,128)(2,1)} %param.22) | copy-start | bytes 786436
  7.2 71.2 %copy-start.2 = (bf16[2048,128]{1,0:T(8,128)(2,1)S(1)}, bf16[2048,128]{1,0:T(8,128)(2,1)}, u32[]{:S(2)}) copy-start(bf16[2048,128]{1,0:T(8,128)(2,1)} %param.17) | copy-start | bytes 1572868
  7.2 68.5 %all-gather.6.cloned.1.call-start = ((), (), s32[]{:S(2)}) async-start(), calls=%async_computation.1 | async-start | bytes 2162688 | tf_op jit(solution)/shard_map/all_gather | solution.py:66
  7.9 195.2 %all-gather.8.cloned.1.call-start = ((), (), s32[]{:S(2)}) async-start(), calls=%async_computation.5 | async-start | bytes 8912896 | tf_op jit(solution)/shard_map/all_gather | solution.py:21
  78.6 5.9 copy-start.7
  81.3 3.4 copy-start.1
  87.0 0.8 copy-start.8
  88.0 5.9 copy-start.7
  90.7 3.4 copy-start.1
  96.4 0.8 copy-start.8
  97.2 285.1 %all-reduce.3.cloned.1.call-start = ((), (), s32[]{:S(2)}) async-start(), calls=%async_computation.2 | async-start | bytes 1048576 | tf_op jit(solution)/shard_map/psum | solution.py:140
  240.7 142.8 %copy-start.4 = (bf16[128,1024]{1,0:T(8,128)(2,1)S(1)}, bf16[128,1024]{1,0:T(8,128)(2,1)}, u32[]{:S(2)}) copy-start(bf16[128,1024]{1,0:T(8,128)(2,1)} %param.22) | copy-start | bytes 786436
  240.7 2.8 copy-start.5
  248.4 2.8 copy-start.5
  256.2 240.6 %reduce-scatter.2.cloned.1.call-start = ((), (), s32[]{:S(2)}) async-start(), calls=%async_computation.3 | async-start | bytes 4325376 | tf_op jit(solution)/shard_map/reduce_scatter | solution.py:154
  386.5 1.2 copy-start.6
  386.6 250.0 %all-reduce.5.cloned.1.call-start = ((), (), s32[]{:S(2)}) async-start(), calls=%async_computation.4 | async-start | bytes 1048576 | tf_op jit(solution)/shard_map/psum | solution.py:152
Sparse Core Ops, SparseCore 0:
  11.2 64.5 all-gather.5
  97.3 105.7 all-gather.7
  256.3 125.9 all-reduce.2
  386.7 110.0 reduce-scatter.1
  500.4 136.1 all-reduce.4
where the time goes:
time: 647 us; the launch traced here: 645 us
  waiting for transfers between devices  492 us (76%)
  blocking collectives  49.7 us (8%)
  other arithmetic  35.1 us (5%)
  matrix products  31.6 us (5%)
  local copies, waits for them, and re-layouts  22 us (3%)
  between operations  14 us (2%)
    psum x1, waiting for transfers between devices, shards(): up_weight_gradient = lax.psum(partial_up_weight, 'row')  138 us
    psum x1, waiting for transfers between devices, shards(): summed_grad = lax.psum(partial_grad, 'pre') * score_scale  126 us
    reduce_scatter x1, waiting for transfers between devices, shards(): lax.psum_scatter(lax.dot_general(columns, grad_latent, (((0,), (0,)), (()...  108 us
    all_gather x1, waiting for transfers between devices, shards(): lax.all_gather(a_down, 'row', axis=0, tiled=True)  64.9 us
    all_gather x1, waiting for transfers between devices, combined_all(): gathered = jax.tree.map(lambda a: lax.all_gather(a, axis), part)  53.7 us
    all_gather x2, blocking collectives, combined_all(): gathered = jax.tree.map(lambda a: lax.all_gather(a, axis), part)  49.7 us
    add x15, other arithmetic, combine_partials(): first_out * first_factor[:, None] + second_out * second_factor[:, None]  22.5 us
  transfers between devices with their start and end apart: 5, of which 5 were waited for; matrix products, arithmetic and copies ran while one was open for 1% of the time, Pallas kernels for 0%

commit v1 on v0

v1 whole, which is shorter than its diff:
```python
import functools
import math

import jax
import jax.numpy as jnp
from jax import lax
from jax.experimental import pallas as pl
from jax.experimental.pallas import tpu as pltpu
from jax.sharding import PartitionSpec as P

HD = 128
RANK = 16
MB = 128
ADAPTER_SCALE = 2.0
DEAD = -1e30
FLOOR = -1e29
TINY = 1e-30
SUBS = 2
MESH = pl.DeviceIdType.MESH
F32 = jnp.float32
BF16 = jnp.bfloat16


def dot(a, b, ca, cb):
    return lax.dot_general(a, b, (((ca,), (cb,)), ((), ())), preferred_element_type=F32)


def remote(src, dst, send_sem, recv_sem, pre, row):
    return pltpu.make_async_remote_copy(
        src_ref=src,
        dst_ref=dst,
        send_sem=send_sem,
        recv_sem=recv_sem,
        device_id=(pre, row),
        device_id_type=MESH,
    )


def picker(ids_ref, students, ranks):
    place = lax.broadcasted_iota(jnp.int32, (ranks, ranks), 0)
    column = lax.broadcasted_iota(jnp.int32, (ranks, ranks), 1)
    wanted = jnp.zeros((ranks, ranks), jnp.int32)
    for s in range(students):
        wanted = jnp.where(place // RANK == s, ids_ref[s] * RANK + place % RANK, wanted)
    return jnp.where(column == wanted, 1.0, 0.0).astype(BF16)


def query_kernel(
    per_student,
    row_count,
    ids_ref,
    a_ref,
    hidden_hbm,
    up_ref,
    base_ref,
    latent_ref,
    query_ref,
    own_up_ref,
    outgoing,
    incoming,
    hidden,
    send_sem,
    recv_sem,
    load_sem,
):
    pre = lax.axis_index("pre")
    row = lax.axis_index("row")
    students = row_count // per_student
    depth = a_ref.shape[0]
    ranks = a_ref.shape[1]
    barrier = pltpu.get_barrier_semaphore()

    def greet(k, carry):
        pl.semaphore_signal(
            barrier, inc=1, device_id=(pre, (row + k) % row_count), device_id_type=MESH
        )
        return carry

    lax.fori_loop(1, row_count, greet, 0)
    load = pltpu.make_async_copy(hidden_hbm, hidden, load_sem)
    load.start()
    pick = picker(ids_ref, students, ranks)
    picked = dot(pick, a_ref[...], 1, 1).astype(BF16)
    for s in range(students):
        outgoing[s] = picked[s * RANK : (s + 1) * RANK]
    pl.semaphore_wait(barrier, row_count - 1)

    def send(k, carry):
        to = (row + k) % row_count
        remote(
            outgoing.at[to // per_student],
            incoming.at[row],
            send_sem.at[k],
            recv_sem.at[row],
            pre,
            to,
        ).start()
        return carry

    lax.fori_loop(1, row_count, send, 0)
    load.wait()
    mine = row // per_student

    def project(k, total):
        source = (row - k + row_count) % row_count
        remote(
            outgoing.at[0], incoming.at[source], send_sem.at[0], recv_sem.at[source], pre, row
        ).wait_recv()
        block = hidden[:, pl.ds(pl.multiple_of(source * depth, depth), depth)]
        return total + dot(incoming[source], block, 1, 1)

    own = dot(outgoing[mine], hidden[:, pl.ds(pl.multiple_of(row * depth, depth), depth)], 1, 1)
    total = lax.fori_loop(1, row_count, project, own)
    latent = total.astype(BF16)
    latent_ref[...] = latent
    place = lax.broadcasted_iota(jnp.int32, (RANK, ranks), 0)
    column = lax.broadcasted_iota(jnp.int32, (RANK, ranks), 1)
    own_pick = jnp.where(column == ids_ref[mine] * RANK + place, 1.0, 0.0).astype(BF16)
    up = dot(own_pick, up_ref[...], 1, 0).astype(BF16)
    own_up_ref[...] = up
    raised = dot(latent, up, 0, 0)
    query_ref[...] = (base_ref[...].astype(F32) + ADAPTER_SCALE * raised).astype(BF16)

    def finish(k, carry):
        remote(
            outgoing.at[0], incoming.at[0], send_sem.at[k], recv_sem.at[0], pre, row
        ).wait_send()
        return carry

    lax.fori_loop(1, row_count, finish, 0)


def split_parts(x, count):
    parts = []
    for _ in range(count):
        part = x.astype(BF16).astype(F32)
        parts.append(part)
        x = x - part
    return parts


def merge(first, second, fold):
    m1, l1, d1, o1, b1, a1 = first
    m2, l2, d2, o2, b2, a2 = second
    m = jnp.maximum(m1, m2)
    f1 = jnp.exp2((m1 - m) * fold)
    f2 = jnp.exp2((m2 - m) * fold)
    w1 = f1 * l1
    w2 = f2 * l2
    total = w1 + w2
    centre = (w1 * d1 + w2 * d2) / jnp.maximum(total, TINY)
    o = f1 * o1 + f2 * o2
    b = f1 * b1 + f2 * b2
    a = f1 * (a1 + (d1 - centre) * b1) + f2 * (a2 + (d2 - centre) * b2)
    return (m, total, centre, o, b, a)


def attention_kernel(
    pre_count,
    row_count,
    per_student,
    ids_ref,
    mask_ref,
    query_ref,
    upstream_ref,
    key_ref,
    value_ref,
    latent_ref,
    up_ref,
    hidden_hbm,
    attended_ref,
    grad_a_ref,
    grad_up_ref,
    hidden,
    q_rows,
    u_rows,
    bias,
    value_key,
    scores,
    local,
    ring_out,
    ring_in,
    fixed,
    term_out,
    term_in,
    att_out,
    att_in,
    quarter_out,
    quarter_in,
    grad_out,
    grad_in,
    up_out,
    up_in,
    raised,
    grad_rows,
    up_rows,
    load_sem,
    ring_send,
    ring_recv,
    term_send,
    term_recv,
    att_send,
    att_recv,
    quarter_send,
    quarter_recv,
    grad_send,
    grad_recv,
    up_send,
    up_recv,
):
    pre = lax.axis_index("pre")
    row = lax.axis_index("row")
    tokens = query_ref.shape[0]
    heads = query_ref.shape[1] // HD
    keys = key_ref.shape[0]
    students = row_count // per_student
    own_rows = heads * tokens // pre_count
    pieces = tokens // own_rows
    sub_rows = own_rows // SUBS
    half = pre_count // 2
    score_scale = 1.0 / math.sqrt(HD)
    fold = score_scale * math.log2(math.e)
    student = row // per_student
    place = row % per_student
    first_row = student * per_student
    depth = grad_a_ref.shape[0]
    width = grad_up_ref.shape[1] // per_student
    barrier = pltpu.get_barrier_semaphore()

    def greet_row(k, carry):
        pl.semaphore_signal(
            barrier, inc=1, device_id=(pre, (row + k) % row_count), device_id_type=MESH
        )
        return carry

    def greet_pre(k, carry):
        pl.semaphore_signal(
            barrier, inc=1, device_id=((pre + k) % pre_count, row), device_id_type=MESH
        )
        return carry

    lax.fori_loop(1, pre_count, greet_pre, 0)
    lax.fori_loop(1, row_count, greet_row, 0)
    load = pltpu.make_async_copy(hidden_hbm, hidden, load_sem)
    load.start()

    value_key[:, :HD] = value_ref[...]
    value_key[:, HD:] = key_ref[...]
    for h in range(heads):
        q_rows[h * tokens : (h + 1) * tokens, :] = query_ref[:, h * HD : (h + 1) * HD]
        u_rows[h * tokens : (h + 1) * tokens, :] = upstream_ref[:, h * HD : (h + 1) * HD]
    for b in range(keys // MB):
        read = jnp.full((8, MB), mask_ref[student, b], jnp.int32)
        bias[:, b * MB : (b + 1) * MB] = jnp.where(read > 0, 0.0, DEAD)
    block = min(256, heads * tokens)
    step = min(512, keys)

    def attend(i, carry):
        rows = pl.ds(pl.multiple_of(i * block, block), block)
        q = q_rows[rows, :]
        u = u_rows[rows, :]
        high = jnp.full((block, HD), FLOOR, F32)
        for j in range(keys // step):
            cols = slice(j * step, (j + 1) * step)
            s = dot(q, key_ref[cols, :], 1, 1) + bias[0:1, cols]
            scores[:, cols] = s
            for g in range(step // HD):
                high = jnp.maximum(high, s[:, g * HD : (g + 1) * HD])
        m = jnp.max(high, axis=1, keepdims=True)
        sums = jnp.zeros((block, HD), F32)
        both = jnp.zeros((block, 2 * HD), F32)
        for j in range(keys // step):
            cols = slice(j * step, (j + 1) * step)
            w = jnp.exp2((scores[:, cols] - m) * fold)
            scores[:, cols] = w
            for g in range(step // HD):
                sums = sums + w[:, g * HD : (g + 1) * HD]
            both = both + dot(w.astype(BF16), value_key[cols, :], 1, 0)
        l = jnp.sum(sums, axis=1, keepdims=True)
        o = both[:, :HD]
        d = jnp.sum(u.astype(F32) * o, axis=1, keepdims=True) / jnp.maximum(l, TINY)
        a = jnp.zeros((block, HD), F32)
        for j in range(keys // step):
            cols = slice(j * step, (j + 1) * step)
            dp = dot(u, value_ref[cols, :], 1, 1)
            g = (scores[:, cols] * (dp - d)).astype(BF16)
            a = a + dot(g, key_ref[cols, :], 1, 0)
        local[0, rows, :] = jnp.broadcast_to(m, (block, HD))
        local[1, rows, :] = jnp.broadcast_to(l, (block, HD))
        local[2, rows, :] = jnp.broadcast_to(d, (block, HD))
        local[3, rows, :] = o
        local[4, rows, :] = both[:, HD:]
        local[5, rows, :] = a
        return carry

    lax.fori_loop(0, heads * tokens // block, attend, 0)

    lane_in = lax.broadcasted_iota(jnp.int32, (HD, 3 * HD), 0)
    lane_out = lax.broadcasted_iota(jnp.int32, (HD, 3 * HD), 1) // HD
    spread = jnp.where(
        (lane_in < 3) & (lane_out == 0)
        | (lane_in >= 3) & (lane_in < 5) & (lane_out == 1)
        | (lane_in >= 5) & (lane_in < 7) & (lane_out == 2),
        1.0,
        0.0,
    ).astype(BF16)
    fixed[...] = spread
    lane = lax.broadcasted_iota(jnp.int32, (sub_rows, HD), 1)

    def local_term(chunk, sub):
        rows = pl.ds(pl.multiple_of(chunk * own_rows + sub * sub_rows, sub_rows), sub_rows)
        return tuple(local[n, rows, :] for n in range(6))

    def arrived(flow, t, sub):
        data = ring_in[flow, t, sub]
        stats = dot(data[:, 3 * HD :], fixed[...], 1, 0)
        return (
            stats[:, :HD],
            stats[:, HD : 2 * HD],
            stats[:, 2 * HD :],
            data[:, :HD].astype(F32),
            data[:, HD : 2 * HD].astype(F32),
            data[:, 2 * HD : 3 * HD].astype(F32),
        )

    def ring_copy(flow, t, sub):
        step_to = 1 if flow == 0 else pre_count - 1
        return remote(
            ring_out.at[flow, t, sub],
            ring_in.at[flow, t, sub],
            ring_send.at[flow, t, sub],
            ring_recv.at[flow, t, sub],
            (pre + step_to) % pre_count,
            row,
        )

    def pass_on(flow, t, sub, term):
        m, l, d, o, b, a = term
        parts = split_parts(m, 3) + split_parts(l, 2) + split_parts(d, 2)
        stats = jnp.zeros((sub_rows, HD), F32)
        for n, part in enumerate(parts):
            stats = jnp.where(lane == n, part, stats)
        ring_out[flow, t, sub, :, :HD] = o.astype(BF16)
        ring_out[flow, t, sub, :, HD : 2 * HD] = b.astype(BF16)
        ring_out[flow, t, sub, :, 2 * HD : 3 * HD] = a.astype(BF16)
        ring_out[flow, t, sub, :, 3 * HD :] = stats.astype(BF16)
        ring_copy(flow, t, sub).start()

    def chunk_of(flow, t):
        if flow == 0:
            return (pre + half - t) % pre_count
        return (pre + half + t) % pre_count

    pl.semaphore_wait(barrier, row_count - 1 + pre_count - 1)
    for sub in range(SUBS):
        pass_on(1, 0, sub, local_term(chunk_of(1, 0), sub))
    for sub in range(SUBS):
        pass_on(0, 1, sub, local_term(chunk_of(0, 1), sub))
    for sub in range(SUBS):
        ring_copy(1, 0, sub).wait_recv()
        pass_on(1, 1, sub, merge(arrived(1, 0, sub), local_term(chunk_of(1, 1), sub), fold))

    def ring_step(t, carry):
        for sub in range(SUBS):
            for flow in (0, 1):
                ring_copy(flow, t - 1, sub).wait_recv()
                term = merge(arrived(flow, t - 1, sub), local_term(chunk_of(flow, t), sub), fold)
                pass_on(flow, t, sub, term)
        return carry

    lax.fori_loop(2, half, ring_step, 0)

    head = pre // pieces
    piece = pre % pieces
    parts = []
    for sub in range(SUBS):
        ring_copy(0, half - 1, sub).wait_recv()
        term = merge(arrived(0, half - 1, sub), local_term(pre, sub), fold)
        ring_copy(1, half - 1, sub).wait_recv()
        m, l, d, o, b, a = merge(term, arrived(1, half - 1, sub), fold)
        inverse = 1.0 / l
        attended = (o * inverse).astype(BF16)
        rows = pl.ds(pl.multiple_of(pre * own_rows + sub * sub_rows, sub_rows), sub_rows)
        u = u_rows[rows, :].astype(F32)
        delta = jnp.sum(u * attended.astype(F32), axis=1, keepdims=True)
        att_out[sub * sub_rows : (sub + 1) * sub_rows, :] = attended
        parts.append((((a + (d - delta) * b) * inverse) * score_scale).astype(BF16))
    grad_q = jnp.concatenate(parts * pieces, axis=0)
    piece_of = lax.broadcasted_iota(jnp.int32, (tokens, HD), 0) // own_rows
    grad_q = jnp.where(piece_of == piece, grad_q.astype(F32), 0.0).astype(BF16)
    up_head = up_ref[:, pl.ds(pl.multiple_of(head * HD, HD), HD)]
    term_out[:RANK, :tokens] = (ADAPTER_SCALE * dot(up_head, grad_q, 1, 1)).astype(BF16)
    term_out[RANK:, :HD] = (ADAPTER_SCALE * dot(latent_ref[...], grad_q, 1, 0)).astype(BF16)

    def term_copy(k):
        to = (pre + k) % pre_count
        return remote(term_out, term_in.at[pre], term_send.at[k], term_recv.at[pre], to, row)

    def att_copy(k):
        to = (pre + k) % pre_count
        return remote(att_out, att_in.at[pre], att_send.at[k], att_recv.at[pre], to, row)

    def send_term(k, carry):
        term_copy((k + half - 1) % (pre_count - 1) + 1).start()
        return carry

    def send_att(k, carry):
        att_copy((k + half - 1) % (pre_count - 1) + 1).start()
        return carry

    lax.fori_loop(0, pre_count - 1, send_term, 0)
    lax.fori_loop(0, pre_count - 1, send_att, 0)
    term_in[pre] = term_out[...]
    att_in[pre] = att_out[...]

    def take_term(k, carry):
        source = (pre + k) % pre_count
        remote(
            term_out, term_in.at[source], term_send.at[0], term_recv.at[source], pre, row
        ).wait_recv()
        return carry

    load.wait()
    lax.fori_loop(1, pre_count, take_term, 0)
    code = jnp.zeros((RANK, tokens), F32)
    for h in range(heads):
        lifted = jnp.zeros((RANK, HD), F32)
        for n in range(pieces):
            code = code + term_in[h * pieces + n, :RANK, :tokens].astype(F32)
            lifted = lifted + term_in[h * pieces + n, RANK:, :HD].astype(F32)
        raised[:, h * HD : (h + 1) * HD] = lifted
    for n in range(per_student):
        quarter_out[n] = raised[:, n * width : (n + 1) * width].astype(BF16)

    def quarter_copy(k):
        to = (place + k) % per_student
        return remote(
            quarter_out.at[to],
            quarter_in.at[place],
            quarter_send.at[k],
            quarter_recv.at[place],
            pre,
            first_row + to,
        )

    for k in range(1, per_student):
        quarter_copy(k).start()
    code = code.astype(BF16)

    def grad_copy(k, to):
        return remote(
            grad_out.at[to], grad_in.at[row], grad_send.at[k], grad_recv.at[row], pre, to
        )

    def send_grad(k, carry):
        to = (row + k) % row_count
        cols = pl.ds(pl.multiple_of(to * depth, depth), depth)
        grad_out[to] = dot(code, hidden[:, cols], 1, 0).astype(BF16)
        grad_copy(k, to).start()
        return carry

    lax.fori_loop(1, row_count, send_grad, 0)
    cols = pl.ds(pl.multiple_of(row * depth, depth), depth)
    grad_in[row] = dot(code, hidden[:, cols], 1, 0).astype(BF16)

    quarter_in[place] = quarter_out[place]
    for k in range(1, per_student):
        source = (place + k) % per_student
        remote(
            quarter_out.at[0],
            quarter_in.at[source],
            quarter_send.at[0],
            quarter_recv.at[source],
            pre,
            row,
        ).wait_recv()
    summed = jnp.zeros((RANK, width), F32)
    for n in range(per_student):
        summed = summed + quarter_in[n].astype(F32)
    up_out[...] = summed.astype(BF16)

    def up_copy(k):
        to = (row + k) % row_count
        return remote(up_out, up_in.at[row], up_send.at[k], up_recv.at[row], pre, to)

    def send_up(k, carry):
        up_copy(k).start()
        return carry

    lax.fori_loop(1, row_count, send_up, 0)
    up_in[row] = up_out[...]

    pick = picker(ids_ref, students, students * RANK)

    def take_grad(k, carry):
        source = (row + k) % row_count
        remote(
            grad_out.at[0], grad_in.at[source], grad_send.at[0], grad_recv.at[source], pre, row
        ).wait_recv()
        return carry

    lax.fori_loop(1, row_count, take_grad, 0)
    for s in range(students):
        block_sum = grad_in[s * per_student].astype(F32)
        for n in range(1, per_student):
            block_sum = block_sum + grad_in[s * per_student + n].astype(F32)
        for n, part in enumerate(split_parts(block_sum, 2)):
            grad_rows[n, s * RANK : (s + 1) * RANK, :] = part.astype(BF16)
    grad_a_ref[...] = dot(grad_rows[0], pick, 0, 0) + dot(grad_rows[1], pick, 0, 0)

    def take_up(k, carry):
        source = (row + k) % row_count
        remote(
            up_out, up_in.at[source], up_send.at[0], up_recv.at[source], pre, row
        ).wait_recv()
        return carry

    lax.fori_loop(1, row_count, take_up, 0)
    for s in range(students):
        for j in range(per_student):
            up_rows[s * RANK : (s + 1) * RANK, j * width : (j + 1) * width] = up_in[
                s * per_student + j
            ]
    grad_up_ref[...] = dot(pick, up_rows[...], 0, 0)

    def take_att(k, carry):
        source = (pre + k) % pre_count
        remote(
            att_out, att_in.at[source], att_send.at[0], att_recv.at[source], pre, row
        ).wait_recv()
        return carry

    lax.fori_loop(1, pre_count, take_att, 0)
    for h in range(heads):
        for n in range(pieces):
            attended_ref[
                n * own_rows : (n + 1) * own_rows, h * HD : (h + 1) * HD
            ] = att_in[h * pieces + n]

    for sub in range(SUBS):
        ring_copy(1, 0, sub).wait_send()

    def ring_done(t, carry):
        for sub in range(SUBS):
            for flow in (0, 1):
                ring_copy(flow, t, sub).wait_send()
        return carry

    lax.fori_loop(1, half, ring_done, 0)

    def pre_done(k, carry):
        term_copy(k).wait_send()
        att_copy(k).wait_send()
        return carry

    lax.fori_loop(1, pre_count, pre_done, 0)
    for k in range(1, per_student):
        quarter_copy(k).wait_send()

    def row_done(k, carry):
        grad_copy(k, (row + k) % row_count).wait_send()
        up_copy(k).wait_send()
        return carry

    lax.fori_loop(1, row_count, row_done, 0)


def vmem():
    return pl.BlockSpec(memory_space=pltpu.VMEM)


def smem():
    return pl.BlockSpec(memory_space=pltpu.SMEM)


def anywhere():
    return pl.BlockSpec(memory_space=pl.ANY)


def shards(
    pre_count,
    row_count,
    hidden_in,
    frozen_query_base,
    k_prefix,
    v_prefix,
    tree_mask,
    adapter_ids,
    a_down,
    up_weight_matrix,
    cotangent,
):
    tokens, width = frozen_query_base.shape
    model = hidden_in.shape[1]
    heads = width // HD
    keys = k_prefix.shape[0]
    depth, ranks = a_down.shape
    students = tree_mask.shape[0]
    per_student = row_count // students
    dma = pltpu.SemaphoreType.DMA
    latent, queries, own_up = pl.pallas_call(
        functools.partial(query_kernel, per_student, row_count),
        out_shape=(
            jax.ShapeDtypeStruct((RANK, tokens), BF16),
            jax.ShapeDtypeStruct((tokens, width), BF16),
            jax.ShapeDtypeStruct((RANK, width), BF16),
        ),
        in_specs=[smem(), vmem(), anywhere(), vmem(), vmem()],
        out_specs=(vmem(), vmem(), vmem()),
        scratch_shapes=[
            pltpu.VMEM((students, RANK, depth), BF16),
            pltpu.VMEM((row_count, RANK, depth), BF16),
            pltpu.VMEM((tokens, model), BF16),
            dma((row_count,)),
            dma((row_count,)),
            dma,
        ],
        compiler_params=pltpu.CompilerParams(collective_id=0, has_side_effects=True),
        name="queries",
    )(adapter_ids, a_down, hidden_in, up_weight_matrix, frozen_query_base)

    rows = heads * tokens
    own_rows = rows // pre_count
    half = pre_count // 2
    quarter = width // per_student
    attended, grad_a, grad_up = pl.pallas_call(
        functools.partial(attention_kernel, pre_count, row_count, per_student),
        out_shape=(
            jax.ShapeDtypeStruct((tokens, width), BF16),
            jax.ShapeDtypeStruct((depth, ranks), F32),
            jax.ShapeDtypeStruct((ranks, width), F32),
        ),
        in_specs=[smem(), smem()] + [vmem()] * 6 + [anywhere()],
        out_specs=(vmem(), vmem(), vmem()),
        scratch_shapes=[
            pltpu.VMEM((tokens, model), BF16),
            pltpu.VMEM((rows, HD), BF16),
            pltpu.VMEM((rows, HD), BF16),
            pltpu.VMEM((8, keys), F32),
            pltpu.VMEM((keys, 2 * HD), BF16),
            pltpu.VMEM((min(256, rows), keys), F32),
            pltpu.VMEM((6, rows, HD), F32),
            pltpu.VMEM((2, half, SUBS, own_rows // SUBS, 4 * HD), BF16),
            pltpu.VMEM((2, half, SUBS, own_rows // SUBS, 4 * HD), BF16),
            pltpu.VMEM((HD, 3 * HD), BF16),
            pltpu.VMEM((2 * RANK, HD), BF16),
            pltpu.VMEM((pre_count, 2 * RANK, HD), BF16),
            pltpu.VMEM((own_rows, HD), BF16),
            pltpu.VMEM((pre_count, own_rows, HD), BF16),
            pltpu.VMEM((per_student, RANK, quarter), BF16),
            pltpu.VMEM((per_student, RANK, quarter), BF16),
            pltpu.VMEM((row_count, RANK, depth), BF16),
            pltpu.VMEM((row_count, RANK, depth), BF16),
            pltpu.VMEM((RANK, quarter), BF16),
            pltpu.VMEM((row_count, RANK, quarter), BF16),
            pltpu.VMEM((RANK, width), F32),
            pltpu.VMEM((2, ranks, depth), BF16),
            pltpu.VMEM((ranks, width), BF16),
            dma,
            dma((2, half, SUBS)),
            dma((2, half, SUBS)),
            dma((pre_count,)),
            dma((pre_count,)),
            dma((pre_count,)),
            dma((pre_count,)),
            dma((per_student,)),
            dma((per_student,)),
            dma((row_count,)),
            dma((row_count,)),
            dma((row_count,)),
            dma((row_count,)),
        ],
        compiler_params=pltpu.CompilerParams(collective_id=1, has_side_effects=True),
        name="attention",
    )(
        adapter_ids,
        tree_mask,
        queries,
        cotangent,
        k_prefix,
        v_prefix,
        latent,
        own_up,
        hidden_in,
    )
    return (attended, grad_a, grad_up)


def solution(mesh):
    in_specs = (
        P("row", None),
        P("row", None),
        P("pre", None),
        P("pre", None),
        P(None, "pre"),
        P(),
        P("row", None),
        P(),
        P("row", None),
    )
    out_specs = (P("row", None), P("row", None), P())
    body = functools.partial(shards, mesh.shape["pre"], mesh.shape["row"])
    return jax.shard_map(body, mesh=mesh, in_specs=in_specs, out_specs=out_specs, check_vma=False)
```

time: 647 us -> 98.6 us (0.15)
  waiting for transfers between devices: 492 us -> 0 us
  Pallas kernels: 0 us -> 92.5 us
  blocking collectives: 49.7 us -> 0 us
  other arithmetic: 35.1 us -> 0 us
  matrix products: 31.6 us -> 0 us
  local copies, waits for them, and re-layouts: 22 us -> 5.12 us
  between operations: 14 us -> 0.65 us
    psum x2 -> x0, waiting for transfers between devices: 264 us -> none  [the longest x1 138 us: shards(): up_weight_gradient = lax.psum(partial_up_weight, 'row')]
    all_gather x2 -> x0, waiting for transfers between devices: 119 us -> none  [the longest x1 64.9 us: shards(): lax.all_gather(a_down, 'row', axis=0, tiled=True)]
    reduce_scatter x1 -> x0, waiting for transfers between devices: 108 us -> none  [shards(): lax.psum_scatter(lax.dot_general(columns, grad_latent, (((0,), (0,)), (()...]
    pallas_call x0 -> x2, Pallas kernels: none -> 92.5 us  [the longest x1 70 us: shards(): pl.pallas_call(functools.partial(attention_kernel, pre_count, row_count,...]
    all_gather x2 -> x0, blocking collectives: 49.7 us -> none  [combined_all(): gathered = jax.tree.map(lambda a: lax.all_gather(a, axis), part)]
    dot_general x12 -> x0, matrix products: 31.6 us -> none  [the longest x4 10.6 us: block_scores(): lax.dot_general(query_rows, key_block, (((1,), (1,)), ((), ())), preferre...]
    add x33 -> x0, other arithmetic: 22.7 us -> none  [the longest x15 22.5 us: combine_partials(): first_out * first_factor[:, None] + second_out * second_factor[:, None]]
    dynamic_slice x18 -> x0, local copies, waits for them, and re-layouts: 12.7 us -> none  [take(): lax.dynamic_index_in_dim(a, source, 0, False)]
  transfers between devices with their start and end apart: 5 -> 0, of which waited for: 5 -> 0; matrix products, arithmetic and copies ran while one was open for 1% -> 0% of each run, Pallas kernels for 0% -> 0%
where the time goes in v1:
time: 98.6 us; the launch traced here: 98.3 us
  Pallas kernels  92.5 us (94%)
  local copies, waits for them, and re-layouts  5.12 us (5%)
    pallas_call x1, Pallas kernels, shards(): pl.pallas_call(functools.partial(attention_kernel, pre_count, row_count,...  70 us
    pallas_call x1, Pallas kernels, shards(): pl.pallas_call(functools.partial(query_kernel, per_student, row_count), o...  22.5 us
    unnamed x3, local copies, waits for them, and re-layouts  5.12 us

profile of v1, /device:TPU:1, one launch (start us, length us, event | category | flops | bytes accessed | tf_op | source)
XLA Modules:
  0.0 98.3 jit_solution(11688075957095568343)
XLA Ops:
  0.6 22.5 %queries.1 = (bf16[16,128]{1,0:T(8,128)(2,1)}, bf16[128,1024]{1,0:T(8,128)(2,1)}, bf16[16,1024]{1,0:T(8,128)(2,1)}) custom-call(s32[8]{0:T(128)} %ids_ref.3, bf16[256,128]{1,0:T(8,128)(2,1)} %a_ref.1, bf16[128,8192]{1,0:T(8,128)(2,1)} %hidden_hbm.3, bf16[128,1024]{1,0:T(8,128)(2,1)} %up_ref.1, bf16[128,1024]{1,0:T(8,128)(2,1)} %base_ref.1), custom_call_target="tpu_custom_call" | custom-call | tf_op jit(solution)/shard_map/queries/pallas_call | solution.py:601
  23.2 70.0 %attention.1 = (bf16[128,1024]{1,0:T(8,128)(2,1)}, f32[256,128]{1,0:T(8,128)}, f32[128,1024]{1,0:T(8,128)}) custom-call(s32[8]{0:T(128)} %ids_ref.3, s32[8,16]{1,0:T(8,128)} %mask_ref.1, bf16[128,1024]{1,0:T(8,128)(2,1)} %get-tuple-element.6.query_ref, bf16[128,1024]{1,0:T(8,128)(2,1)} %upstream_ref.1, bf16[2048,128]{1,0:T(8,128)(2,1)} %key_ref.1, ...), custom_call_target="tpu_custom_call" | custom-call | tf_op jit(solution)/shard_map/attention/pallas_call | solution.py:626
  93.1 1.7 %copy.15 = bf16[128,1024]{1,0:T(8,128)(2,1)} copy(bf16[128,1024]{1,0:T(8,128)(2,1)} %get-tuple-element.12) | data formatting | bytes 524288
  94.8 1.6 %copy.16 = f32[256,128]{1,0:T(8,128)} copy(f32[256,128]{1,0:T(8,128)} %get-tuple-element.13) | data formatting | bytes 262144
  96.4 1.9 %copy.17 = f32[128,1024]{1,0:T(8,128)} copy(f32[128,1024]{1,0:T(8,128)} %get-tuple-element.14) | data formatting | bytes 1048576

commit v2 on v1

v2 whole, which is shorter than its diff:
```python
import functools
import math

import jax
import jax.numpy as jnp
from jax import lax
from jax.experimental import pallas as pl
from jax.experimental.pallas import tpu as pltpu
from jax.sharding import PartitionSpec as P

HD = 128
RANK = 16
MB = 128
ADAPTER_SCALE = 2.0
DEAD = -1e30
FLOOR = -1e29
TINY = 1e-30
BLOCK = 512
LOG2E = math.log2(math.e)
MESH = pl.DeviceIdType.MESH
F32 = jnp.float32
BF16 = jnp.bfloat16


def dot(a, b, ca, cb):
    return lax.dot_general(a, b, (((ca,), (cb,)), ((), ())), preferred_element_type=F32)


def remote(src, dst, send_sem, recv_sem, pre, row):
    return pltpu.make_async_remote_copy(
        src_ref=src,
        dst_ref=dst,
        send_sem=send_sem,
        recv_sem=recv_sem,
        device_id=(pre, row),
        device_id_type=MESH,
    )


def plane_offsets(row_count):
    extent = (4, 4, 2) if row_count == 32 else (1, row_count // 2, 2)
    around = lambda n, size: min(n, size - n)
    offsets = [
        (around(x, extent[0]) + around(y, extent[1]), x, y, c)
        for x in range(extent[0])
        for y in range(extent[1])
        for c in range(extent[2])
    ]
    return extent, [o[1:] for o in sorted(offsets, key=lambda o: -o[0]) if o[1:] != (0, 0, 0)]


def plane_peer(row, extent, offset):
    _, ys, cs = extent
    x = (row // (ys * cs) + offset[0]) % extent[0]
    y = (row // cs % ys + offset[1]) % ys
    return (x * ys + y) * cs + (row % cs + offset[2]) % cs


def line_offsets(count):
    return sorted(range(1, count), key=lambda k: -min(k, count - k))


def picker(ids_ref, students, ranks):
    place = lax.broadcasted_iota(jnp.int32, (ranks, ranks), 0)
    column = lax.broadcasted_iota(jnp.int32, (ranks, ranks), 1)
    wanted = jnp.zeros((ranks, ranks), jnp.int32)
    for s in range(students):
        wanted = jnp.where(place // RANK == s, ids_ref[s] * RANK + place % RANK, wanted)
    return jnp.where(column == wanted, 1.0, 0.0).astype(BF16)


def query_kernel(
    per_student,
    row_count,
    ids_ref,
    a_ref,
    hidden_hbm,
    up_ref,
    base_ref,
    latent_ref,
    query_ref,
    own_up_ref,
    outgoing,
    incoming,
    hidden,
    send_sem,
    recv_sem,
    load_sem,
):
    pre = lax.axis_index("pre")
    row = lax.axis_index("row")
    students = row_count // per_student
    depth = a_ref.shape[0]
    ranks = a_ref.shape[1]
    barrier = pltpu.get_barrier_semaphore()

    def greet(k, carry):
        pl.semaphore_signal(
            barrier, inc=1, device_id=(pre, (row + k) % row_count), device_id_type=MESH
        )
        return carry

    lax.fori_loop(1, row_count, greet, 0)
    load = pltpu.make_async_copy(hidden_hbm, hidden, load_sem)
    load.start()
    pick = picker(ids_ref, students, ranks)
    picked = dot(pick, a_ref[...], 1, 1).astype(BF16)
    for s in range(students):
        outgoing[s] = picked[s * RANK : (s + 1) * RANK]
    pl.semaphore_wait(barrier, row_count - 1)

    extent, offsets = plane_offsets(row_count)
    copies = []
    for k, offset in enumerate(offsets):
        to = plane_peer(row, extent, offset)
        copies.append(
            remote(
                outgoing.at[to // per_student],
                incoming.at[row],
                send_sem.at[k],
                recv_sem.at[row],
                pre,
                to,
            )
        )
        copies[-1].start()
    load.wait()
    mine = row // per_student

    def project(k, total):
        source = (row - k + row_count) % row_count
        remote(
            outgoing.at[0], incoming.at[source], send_sem.at[0], recv_sem.at[source], pre, row
        ).wait_recv()
        block = hidden[:, pl.ds(pl.multiple_of(source * depth, depth), depth)]
        return total + dot(incoming[source], block, 1, 1)

    own = dot(outgoing[mine], hidden[:, pl.ds(pl.multiple_of(row * depth, depth), depth)], 1, 1)
    total = lax.fori_loop(1, row_count, project, own)
    latent = total.astype(BF16)
    latent_ref[...] = latent
    place = lax.broadcasted_iota(jnp.int32, (RANK, ranks), 0)
    column = lax.broadcasted_iota(jnp.int32, (RANK, ranks), 1)
    own_pick = jnp.where(column == ids_ref[mine] * RANK + place, 1.0, 0.0).astype(BF16)
    up = dot(own_pick, up_ref[...], 1, 0).astype(BF16)
    own_up_ref[...] = up
    raised = dot(latent, up, 0, 0)
    query_ref[...] = (base_ref[...].astype(F32) + ADAPTER_SCALE * raised).astype(BF16)

    for copy in copies:
        copy.wait_send()


def split_parts(x, count):
    parts = []
    for _ in range(count):
        part = x.astype(BF16).astype(F32)
        parts.append(part)
        x = x - part
    return parts


def attention_kernel(
    pre_count,
    row_count,
    per_student,
    mask_ref,
    query_ref,
    upstream_ref,
    key_ref,
    value_ref,
    latent_ref,
    up_ref,
    hidden_hbm,
    attended_ref,
    grad_ref,
    raised_ref,
    hidden,
    q_rows,
    u_rows,
    bias,
    value_key,
    weights,
    high_rows,
    delta_rows,
    local,
    part,
    stat,
    stat_out,
    stat_in,
    chain_out,
    chain_in,
    odd_out,
    odd_in,
    term_out,
    term_in,
    att_in,
    quarter_out,
    quarter_in,
    grad_out,
    grad_in,
    up_out,
    up_in,
    raised,
    load_sem,
    stat_send,
    stat_recv,
    chain_send,
    chain_recv,
    odd_send,
    odd_recv,
    term_send,
    term_recv,
    att_send,
    att_recv,
    quarter_send,
    quarter_recv,
    grad_send,
    grad_recv,
    up_send,
    up_recv,
):
    pre = lax.axis_index("pre")
    row = lax.axis_index("row")
    tokens = query_ref.shape[0]
    heads = query_ref.shape[1] // HD
    keys = key_ref.shape[0]
    own_rows = heads * tokens // pre_count
    pieces = tokens // own_rows
    half = pre_count // 2
    steps = half // 2
    score_scale = 1.0 / math.sqrt(HD)
    fold = score_scale * LOG2E
    student = row // per_student
    place = row % per_student
    first_row = student * per_student
    depth = grad_out.shape[2]
    width = heads * HD // per_student
    extent, plane = plane_offsets(row_count)
    line = line_offsets(pre_count)
    barrier = pltpu.get_barrier_semaphore()

    for k in line:
        pl.semaphore_signal(
            barrier, inc=1, device_id=((pre + k) % pre_count, row), device_id_type=MESH
        )
    for offset in plane:
        pl.semaphore_signal(
            barrier, inc=1, device_id=(pre, plane_peer(row, extent, offset)), device_id_type=MESH
        )
    load = pltpu.make_async_copy(hidden_hbm, hidden, load_sem)
    load.start()

    value_key[:, :HD] = value_ref[...]
    value_key[:, HD:] = key_ref[...]
    for h in range(heads):
        q_rows[h * tokens : (h + 1) * tokens, :] = query_ref[:, h * HD : (h + 1) * HD]
        u_rows[h * tokens : (h + 1) * tokens, :] = upstream_ref[:, h * HD : (h + 1) * HD]
    for b in range(keys // MB):
        read = jnp.full((8, MB), mask_ref[student, b], jnp.int32)
        bias[:, b * MB : (b + 1) * MB] = jnp.where(read > 0, 0.0, DEAD)
    block = min(BLOCK, heads * tokens)
    step = min(512, keys)
    lane = lax.broadcasted_iota(jnp.int32, (tokens, HD), 1)
    stat[...] = jnp.zeros((tokens, HD), F32)

    def forward(i, carry):
        rows = pl.ds(pl.multiple_of(i * block, block), block)
        q = q_rows[rows, :]
        high = jnp.full((block, HD), FLOOR, F32)
        for j in range(keys // step):
            cols = slice(j * step, (j + 1) * step)
            s = dot(q, key_ref[cols, :], 1, 1) + bias[0:1, cols]
            weights[rows, cols] = s
            for g in range(step // HD):
                high = jnp.maximum(high, s[:, g * HD : (g + 1) * HD])
        m = jnp.max(high, axis=1, keepdims=True)
        sums = jnp.zeros((block, HD), F32)
        both = jnp.zeros((block, 2 * HD), F32)
        for j in range(keys // step):
            cols = slice(j * step, (j + 1) * step)
            w = jnp.exp2((weights[rows, cols] - m) * fold)
            weights[rows, cols] = w
            for g in range(step // HD):
                sums = sums + w[:, g * HD : (g + 1) * HD]
            both = both + dot(w.astype(BF16), value_key[cols, :], 1, 0)
        l = jnp.maximum(jnp.sum(sums, axis=1, keepdims=True), TINY)
        o = both[:, :HD]
        d = jnp.sum(u_rows[rows, :].astype(F32) * o, axis=1, keepdims=True) / l
        lse = m * fold + jnp.log(l) * LOG2E
        high_rows[rows, :] = jnp.broadcast_to(m * fold, (block, HD))
        delta_rows[rows, :] = jnp.broadcast_to(d, (block, HD))
        local[0, rows, :] = o
        local[1, rows, :] = both[:, HD:]
        table = stat[...]
        for n in range(block // tokens):
            h = i * (block // tokens) + n
            piece_rows = slice(n * tokens, (n + 1) * tokens)
            table = jnp.where(lane == h, lse[piece_rows], table)
            table = jnp.where(lane == heads + h, d[piece_rows], table)
        stat[...] = table
        return carry

    lax.fori_loop(0, heads * tokens // block, forward, 0)

    stat_out[...] = stat[...].T[: 2 * heads]
    stat_in[pre] = stat_out[...]
    pl.semaphore_wait(barrier, row_count - 1 + pre_count - 1)

    def line_copies(source, landing, send_sem, recv_sem):
        return [
            remote(
                source,
                landing.at[pre],
                send_sem.at[n],
                recv_sem.at[pre],
                (pre + k) % pre_count,
                row,
            )
            for n, k in enumerate(line)
        ]

    def take_line(source, landing, send_sem, recv_sem):
        for k in reversed(line):
            origin = (pre + k) % pre_count
            remote(
                source, landing.at[origin], send_sem.at[0], recv_sem.at[origin], pre, row
            ).wait_recv()

    stat_copies = line_copies(stat_out, stat_in, stat_send, stat_recv)
    for copy in stat_copies:
        copy.start()

    def backward(i, carry):
        rows = pl.ds(pl.multiple_of(i * block, block), block)
        u = u_rows[rows, :]
        d = delta_rows[rows, :]
        a = jnp.zeros((block, HD), F32)
        for j in range(keys // step):
            cols = slice(j * step, (j + 1) * step)
            dp = dot(u, value_ref[cols, :], 1, 1)
            w = weights[rows, cols]
            g = [
                (w[:, n * HD : (n + 1) * HD] * (dp[:, n * HD : (n + 1) * HD] - d)).astype(BF16)
                for n in range(step // HD)
            ]
            a = a + dot(jnp.concatenate(g, axis=1), key_ref[cols, :], 1, 0)
        local[2, rows, :] = a
        return carry

    lax.fori_loop(0, heads * tokens // block, backward, 0)

    take_line(stat_out, stat_in, stat_send, stat_recv)
    top = stat_in[0, :heads]
    for n in range(1, pre_count):
        top = jnp.maximum(top, stat_in[n, :heads])
    mass = jnp.zeros((heads, tokens), F32)
    mean = jnp.zeros((heads, tokens), F32)
    for n in range(pre_count):
        share = jnp.exp2(stat_in[n, :heads] - top)
        mass = mass + share
        mean = mean + share * stat_in[n, heads:]
    stat[:heads, :] = top + jnp.log(mass) * LOG2E
    stat[heads : 2 * heads, :] = mean / mass
    table = stat[...].T
    for h in range(heads):
        rows = slice(h * tokens, (h + 1) * tokens)
        factor = jnp.exp2(high_rows[rows, :] - table[:, h : h + 1])
        shift = delta_rows[rows, :] - table[:, heads + h : heads + h + 1]
        part[0, rows, :] = (local[2, rows, :] + shift * local[1, rows, :]) * (factor * score_scale)
        part[1, rows, :] = local[0, rows, :] * factor

    def own_part(which, flow, distance):
        chunk = (pre + (distance if flow == 0 else pre_count - distance)) % pre_count
        return part[which, pl.ds(pl.multiple_of(chunk * own_rows, own_rows), own_rows), :]

    def hop(flow, distance):
        return (pre + (distance if flow == 0 else pre_count - distance)) % pre_count

    def chain_copy(flow, t, which):
        return remote(
            chain_out.at[flow, t, which],
            chain_in.at[flow, t, which],
            chain_send.at[flow, t, which],
            chain_recv.at[flow, t, which],
            hop(flow, 2),
            row,
        )

    def odd_copy(flow, t, which):
        return remote(
            odd_out.at[flow, t, which],
            odd_in.at[flow, t, which],
            odd_send.at[flow, t, which],
            odd_recv.at[flow, t, which],
            hop(flow, 1),
            row,
        )

    sent = []
    for t in range(steps):
        for which in (0, 1):
            if t == 0:
                chain_out[1, 0, which] = own_part(which, 1, half).astype(BF16)
                sent.append(chain_copy(1, 0, which))
                sent[-1].start()
            for flow in (0, 1):
                odd_out[flow, t, which] = own_part(which, flow, half - 1 - 2 * t).astype(BF16)
                sent.append(odd_copy(flow, t, which))
                sent[-1].start()
    for t in range(1, steps):
        for which in (0, 1):
            for flow in (0, 1):
                total = own_part(which, flow, half - 2 * t)
                odd_copy(flow, t - 1, which).wait_recv()
                total = total + odd_in[flow, t - 1, which].astype(F32)
                if flow == 1 or t > 1:
                    chain_copy(flow, t - 1, which).wait_recv()
                    total = total + chain_in[flow, t - 1, which].astype(F32)
                chain_out[flow, t, which] = total.astype(BF16)
                sent.append(chain_copy(flow, t, which))
                sent[-1].start()

    head = pre // pieces
    piece = pre % pieces
    results = []
    for which in (0, 1):
        total = own_part(which, 0, 0)
        for flow in (0, 1):
            odd_copy(flow, steps - 1, which).wait_recv()
            total = total + odd_in[flow, steps - 1, which].astype(F32)
            if flow == 1 or steps > 1:
                chain_copy(flow, steps - 1, which).wait_recv()
                total = total + chain_in[flow, steps - 1, which].astype(F32)
        results.append(total.astype(BF16))
        if which == 0:
            grad_q = jnp.concatenate([results[0]] * pieces, axis=0)
            piece_of = lax.broadcasted_iota(jnp.int32, (tokens, HD), 0) // own_rows
            grad_q = jnp.where(piece_of == piece, grad_q.astype(F32), 0.0).astype(BF16)
            up_head = up_ref[:, pl.ds(pl.multiple_of(head * HD, HD), HD)]
            term_out[:RANK, :] = (ADAPTER_SCALE * dot(up_head, grad_q, 1, 1)).astype(BF16)
            term_out[RANK:, :] = (ADAPTER_SCALE * dot(latent_ref[...], grad_q, 1, 0)).astype(BF16)
            term_copies = line_copies(term_out, term_in, term_send, term_recv)
            for copy in term_copies:
                copy.start()
            term_in[pre] = term_out[...]
    att_in[pre] = results[1]

    stride = max(pre_count // 4, 1)
    far = [k for k in (2 * stride, stride, 3 * stride) if k < pre_count]
    near = [k if k <= stride // 2 else k - stride for k in range(1, stride)]

    def att_copy(slot, n, k):
        return remote(
            att_in.at[slot],
            att_in.at[slot],
            att_send.at[n],
            att_recv.at[slot],
            (pre + k + pre_count) % pre_count,
            row,
        )

    att_copies = [att_copy(pre, n, k) for n, k in enumerate(far)]
    for copy in att_copies:
        copy.start()

    load.wait()
    take_line(term_out, term_in, term_send, term_recv)
    code = jnp.zeros((RANK, tokens), F32)
    for h in range(heads):
        lifted = jnp.zeros((RANK, HD), F32)
        for n in range(pieces):
            code = code + term_in[h * pieces + n, :RANK, :].astype(F32)
            lifted = lifted + term_in[h * pieces + n, RANK:, :].astype(F32)
        raised[:, h * HD : (h + 1) * HD] = lifted
    for n in range(per_student):
        quarter_out[n] = raised[:, n * width : (n + 1) * width].astype(BF16)

    def quarter_copy(k):
        to = (place + k) % per_student
        return remote(
            quarter_out.at[to],
            quarter_in.at[place],
            quarter_send.at[k],
            quarter_recv.at[place],
            pre,
            first_row + to,
        )

    for k in range(1, per_student):
        quarter_copy(k).start()
    quarter_in[place] = quarter_out[place]
    code = code.astype(BF16)

    grad_copies = []
    for n, offset in enumerate(plane):
        to = plane_peer(row, extent, offset)
        cols = pl.ds(pl.multiple_of(to * depth, depth), depth)
        grad_out[to] = dot(code, hidden[:, cols], 1, 0).astype(BF16)
        grad_copies.append(
            remote(grad_out.at[to], grad_in.at[row], grad_send.at[n], grad_recv.at[row], pre, to)
        )
        grad_copies[-1].start()
    cols = pl.ds(pl.multiple_of(row * depth, depth), depth)
    grad_in[row] = dot(code, hidden[:, cols], 1, 0).astype(BF16)

    for k in range(1, per_student):
        origin = (place + k) % per_student
        remote(
            quarter_out.at[0],
            quarter_in.at[origin],
            quarter_send.at[0],
            quarter_recv.at[origin],
            pre,
            row,
        ).wait_recv()
    summed = jnp.zeros((RANK, width), F32)
    for n in range(per_student):
        summed = summed + quarter_in[n].astype(F32)
    up_out[...] = summed.astype(BF16)
    up_copies = []
    for n, offset in enumerate(plane):
        to = plane_peer(row, extent, offset)
        up_copies.append(
            remote(up_out, up_in.at[row], up_send.at[n], up_recv.at[row], pre, to)
        )
        up_copies[-1].start()
    up_in[row] = up_out[...]

    def slot_wait(landing, slot, send_sem, recv_sem):
        remote(
            landing.at[slot], landing.at[slot], send_sem.at[0], recv_sem.at[slot], pre, row
        ).wait_recv()

    for k in far:
        slot_wait(att_in, (pre + k) % pre_count, att_send, att_recv)
    for k in near:
        for n in range(len(far) + 1):
            slot = (pre + n * stride) % pre_count
            att_copies.append(att_copy(slot, len(att_copies), k))
            att_copies[-1].start()

    def take_grad(k, carry):
        slot_wait(grad_in, (row + k) % row_count, grad_send, grad_recv)
        return carry

    lax.fori_loop(1, row_count, take_grad, 0)
    grad_ref[...] = grad_in[...]
    for k in near:
        for n in range(len(far) + 1):
            slot = (pre - k + n * stride + pre_count) % pre_count
            slot_wait(att_in, slot, att_send, att_recv)
    attended_ref[...] = att_in[...]

    def take_up(k, carry):
        slot_wait(up_in, (row + k) % row_count, up_send, up_recv)
        return carry

    lax.fori_loop(1, row_count, take_up, 0)
    raised_ref[...] = up_in[...]

    for copy in stat_copies + sent + term_copies + att_copies + grad_copies + up_copies:
        copy.wait_send()
    for k in range(1, per_student):
        quarter_copy(k).wait_send()


def output_kernel(
    per_student, ids_ref, att_ref, grad_ref, raised_ref, attended_ref, grad_a_ref, grad_up_ref, rows, ups
):
    count, own_rows, _ = att_ref.shape
    tokens = attended_ref.shape[0]
    pieces = tokens // own_rows
    students = grad_ref.shape[0] // per_student
    width = raised_ref.shape[2]
    pick = picker(ids_ref, students, students * RANK)
    for s in range(students):
        block_sum = grad_ref[s * per_student].astype(F32)
        for n in range(1, per_student):
            block_sum = block_sum + grad_ref[s * per_student + n].astype(F32)
        for n, piece in enumerate(split_parts(block_sum, 2)):
            rows[n, s * RANK : (s + 1) * RANK, :] = piece.astype(BF16)
        for j in range(per_student):
            ups[s * RANK : (s + 1) * RANK, j * width : (j + 1) * width] = raised_ref[
                s * per_student + j
            ]
    grad_a_ref[...] = dot(rows[0], pick, 0, 0) + dot(rows[1], pick, 0, 0)
    grad_up_ref[...] = dot(pick, ups[...], 0, 0)
    for c in range(count):
        h, n = c // pieces, c % pieces
        attended_ref[n * own_rows : (n + 1) * own_rows, h * HD : (h + 1) * HD] = att_ref[c]


def vmem():
    return pl.BlockSpec(memory_space=pltpu.VMEM)


def smem():
    return pl.BlockSpec(memory_space=pltpu.SMEM)


def anywhere():
    return pl.BlockSpec(memory_space=pl.ANY)


def shards(
    pre_count,
    row_count,
    hidden_in,
    frozen_query_base,
    k_prefix,
    v_prefix,
    tree_mask,
    adapter_ids,
    a_down,
    up_weight_matrix,
    cotangent,
):
    tokens, width = frozen_query_base.shape
    model = hidden_in.shape[1]
    heads = width // HD
    keys = k_prefix.shape[0]
    depth, ranks = a_down.shape
    students = tree_mask.shape[0]
    per_student = row_count // students
    dma = pltpu.SemaphoreType.DMA
    latent, queries, own_up = pl.pallas_call(
        functools.partial(query_kernel, per_student, row_count),
        out_shape=(
            jax.ShapeDtypeStruct((RANK, tokens), BF16),
            jax.ShapeDtypeStruct((tokens, width), BF16),
            jax.ShapeDtypeStruct((RANK, width), BF16),
        ),
        in_specs=[smem(), vmem(), anywhere(), vmem(), vmem()],
        out_specs=(vmem(), vmem(), vmem()),
        scratch_shapes=[
            pltpu.VMEM((students, RANK, depth), BF16),
            pltpu.VMEM((row_count, RANK, depth), BF16),
            pltpu.VMEM((tokens, model), BF16),
            dma((row_count,)),
            dma((row_count,)),
            dma,
        ],
        compiler_params=pltpu.CompilerParams(collective_id=0, has_side_effects=True),
        name="queries",
    )(adapter_ids, a_down, hidden_in, up_weight_matrix, frozen_query_base)

    rows = heads * tokens
    own_rows = rows // pre_count
    steps = pre_count // 4
    quarter = width // per_student
    ring = (2, steps, 2)
    att, grad, raised = pl.pallas_call(
        functools.partial(attention_kernel, pre_count, row_count, per_student),
        out_shape=(
            jax.ShapeDtypeStruct((pre_count, own_rows, HD), BF16),
            jax.ShapeDtypeStruct((row_count, RANK, depth), BF16),
            jax.ShapeDtypeStruct((row_count, RANK, quarter), BF16),
        ),
        in_specs=[smem()] + [vmem()] * 6 + [anywhere()],
        out_specs=(vmem(), vmem(), vmem()),
        scratch_shapes=[
            pltpu.VMEM((tokens, model), BF16),
            pltpu.VMEM((rows, HD), BF16),
            pltpu.VMEM((rows, HD), BF16),
            pltpu.VMEM((8, keys), F32),
            pltpu.VMEM((keys, 2 * HD), BF16),
            pltpu.VMEM((rows, keys), F32),
            pltpu.VMEM((rows, HD), F32),
            pltpu.VMEM((rows, HD), F32),
            pltpu.VMEM((3, rows, HD), F32),
            pltpu.VMEM((2, rows, HD), F32),
            pltpu.VMEM((tokens, HD), F32),
            pltpu.VMEM((2 * heads, tokens), F32),
            pltpu.VMEM((pre_count, 2 * heads, tokens), F32),
            pltpu.VMEM(ring + (own_rows, HD), BF16),
            pltpu.VMEM(ring + (own_rows, HD), BF16),
            pltpu.VMEM(ring + (own_rows, HD), BF16),
            pltpu.VMEM(ring + (own_rows, HD), BF16),
            pltpu.VMEM((2 * RANK, HD), BF16),
            pltpu.VMEM((pre_count, 2 * RANK, HD), BF16),
            pltpu.VMEM((pre_count, own_rows, HD), BF16),
            pltpu.VMEM((per_student, RANK, quarter), BF16),
            pltpu.VMEM((per_student, RANK, quarter), BF16),
            pltpu.VMEM((row_count, RANK, depth), BF16),
            pltpu.VMEM((row_count, RANK, depth), BF16),
            pltpu.VMEM((RANK, quarter), BF16),
            pltpu.VMEM((row_count, RANK, quarter), BF16),
            pltpu.VMEM((RANK, width), F32),
            dma,
            dma((pre_count,)),
            dma((pre_count,)),
            dma(ring),
            dma(ring),
            dma(ring),
            dma(ring),
            dma((pre_count,)),
            dma((pre_count,)),
            dma((pre_count,)),
            dma((pre_count,)),
            dma((per_student,)),
            dma((per_student,)),
            dma((row_count,)),
            dma((row_count,)),
            dma((row_count,)),
            dma((row_count,)),
        ],
        compiler_params=pltpu.CompilerParams(collective_id=1, has_side_effects=True),
        name="attention",
    )(tree_mask, queries, cotangent, k_prefix, v_prefix, latent, own_up, hidden_in)
    return pl.pallas_call(
        functools.partial(output_kernel, per_student),
        out_shape=(
            jax.ShapeDtypeStruct((tokens, width), BF16),
            jax.ShapeDtypeStruct((depth, ranks), F32),
            jax.ShapeDtypeStruct((ranks, width), F32),
        ),
        in_specs=[smem()] + [vmem()] * 3,
        out_specs=(vmem(), vmem(), vmem()),
        scratch_shapes=[
            pltpu.VMEM((2, ranks, depth), BF16),
            pltpu.VMEM((ranks, width), BF16),
        ],
        name="outputs",
    )(adapter_ids, att, grad, raised)


def solution(mesh):
    in_specs = (
        P("row", None),
        P("row", None),
        P("pre", None),
        P("pre", None),
        P(None, "pre"),
        P(),
        P("row", None),
        P(),
        P("row", None),
    )
    out_specs = (P("row", None), P("row", None), P())
    body = functools.partial(shards, mesh.shape["pre"], mesh.shape["row"])
    return jax.shard_map(body, mesh=mesh, in_specs=in_specs, out_specs=out_specs, check_vma=False)
```

time: 98.6 us -> 86.1 us (0.87)
  Pallas kernels: 92.5 us -> 84.9 us
  local copies, waits for them, and re-layouts: 5.12 us -> 0 us
    pallas_call x1, Pallas kernels: 70 us -> 59.4 us  [shards(): pl.pallas_call(functools.partial(attention_kernel, pre_count, row_count,...]
    unnamed x3 -> x0, local copies, waits for them, and re-layouts: 5.12 us -> none
    pallas_call x0 -> x1, Pallas kernels: none -> 2.33 us  [shards(): pl.pallas_call(functools.partial(output_kernel, per_student), out_shape=(...]
where the time goes in v2:
time: 86.1 us; the launch traced here: 85.5 us
  Pallas kernels  84.9 us (99%)
    pallas_call x1, Pallas kernels, shards(): pl.pallas_call(functools.partial(attention_kernel, pre_count, row_count,...  59.4 us
    pallas_call x1, Pallas kernels, shards(): pl.pallas_call(functools.partial(query_kernel, per_student, row_count), o...  23.1 us
    pallas_call x1, Pallas kernels, shards(): pl.pallas_call(functools.partial(output_kernel, per_student), out_shape=(...  2.33 us

profile of v2, /device:TPU:1, one launch (start us, length us, event | category | flops | bytes accessed | tf_op | source)
XLA Modules:
  0.0 85.5 jit_solution(3016657058081925999)
XLA Ops:
  0.6 23.1 %queries.1 = (bf16[16,128]{1,0:T(8,128)(2,1)}, bf16[128,1024]{1,0:T(8,128)(2,1)}, bf16[16,1024]{1,0:T(8,128)(2,1)}) custom-call(s32[8]{0:T(128)} %ids_ref.3, bf16[256,128]{1,0:T(8,128)(2,1)} %a_ref.1, bf16[128,8192]{1,0:T(8,128)(2,1)} %hidden_hbm.3, bf16[128,1024]{1,0:T(8,128)(2,1)} %up_ref.1, bf16[128,1024]{1,0:T(8,128)(2,1)} %base_ref.1), custom_call_target="tpu_custom_call" | custom-call | tf_op jit(solution)/shard_map/queries/pallas_call | solution.py:627
  23.8 59.4 %attention.1 = (bf16[16,64,128]{2,1,0:T(8,128)(2,1)}, bf16[32,16,256]{2,1,0:T(8,128)(2,1)}, bf16[32,16,256]{2,1,0:T(8,128)(2,1)}) custom-call(s32[8,16]{1,0:T(8,128)} %mask_ref.1, bf16[128,1024]{1,0:T(8,128)(2,1)} %get-tuple-element.9.query_ref, bf16[128,1024]{1,0:T(8,128)(2,1)} %upstream_ref.1, bf16[2048,128]{1,0:T(8,128)(2,1)} %key_ref.1, ...), custom_call_target="tpu_custom_call" | custom-call | tf_op jit(solution)/shard_map/attention/pallas_call | solution.py:653
  83.2 2.3 %outputs.1 = (bf16[128,1024]{1,0:T(8,128)(2,1)}, f32[256,128]{1,0:T(8,128)}, f32[128,1024]{1,0:T(8,128)}) custom-call(s32[8]{0:T(128)} %ids_ref.3, bf16[16,64,128]{2,1,0:T(8,128)(2,1)} %get-tuple-element.12.att_ref, bf16[32,16,256]{2,1,0:T(8,128)(2,1)} %get-tuple-element.13.grad_ref, bf16[32,16,256]{2,1,0:T(8,128)(2,1)} %get-tuple-element.14.raised_ref), custom_call_target="tpu_custom_call" | custom-call | tf_op jit(solution)/shard_map/outputs/pallas_call | solution.py:711

commit v3 on v2

--- a/solution.py
+++ b/solution.py
@@ -15,7 +15,7 @@
 DEAD = -1e30
 FLOOR = -1e29
 TINY = 1e-30
-BLOCK = 512
+STEP = 512
 LOG2E = math.log2(math.e)
 MESH = pl.DeviceIdType.MESH
 F32 = jnp.float32
@@ -73,16 +73,19 @@
     per_student,
     row_count,
     ids_ref,
-    a_ref,
+    a_hbm,
     hidden_hbm,
-    up_ref,
-    base_ref,
+    up_hbm,
+    base_hbm,
     latent_ref,
     query_ref,
     own_up_ref,
     outgoing,
     incoming,
+    a_rows,
     hidden,
+    up_rows,
+    base_rows,
     send_sem,
     recv_sem,
     load_sem,
@@ -90,8 +93,7 @@
     pre = lax.axis_index("pre")
     row = lax.axis_index("row")
     students = row_count // per_student
-    depth = a_ref.shape[0]
-    ranks = a_ref.shape[1]
+    depth, ranks = a_hbm.shape
     barrier = pltpu.get_barrier_semaphore()
 
     def greet(k, carry):
@@ -101,22 +103,30 @@
         return carry
 
     lax.fori_loop(1, row_count, greet, 0)
-    load = pltpu.make_async_copy(hidden_hbm, hidden, load_sem)
-    load.start()
+    loads = [
+        pltpu.make_async_copy(source, landing, load_sem.at[n])
+        for n, (source, landing) in enumerate(
+            ((a_hbm, a_rows), (hidden_hbm, hidden), (up_hbm, up_rows), (base_hbm, base_rows))
+        )
+    ]
+    for copy in loads:
+        copy.start()
     pick = picker(ids_ref, students, ranks)
-    picked = dot(pick, a_ref[...], 1, 1).astype(BF16)
+    loads[0].wait()
+    picked = dot(pick, a_rows[...], 1, 1).astype(BF16)
     for s in range(students):
         outgoing[s] = picked[s * RANK : (s + 1) * RANK]
     pl.semaphore_wait(barrier, row_count - 1)
 
     extent, offsets = plane_offsets(row_count)
+    own_cols = pl.ds(pl.multiple_of(row * depth, depth), depth)
     copies = []
     for k, offset in enumerate(offsets):
         to = plane_peer(row, extent, offset)
         copies.append(
             remote(
                 outgoing.at[to // per_student],
-                incoming.at[row],
+                incoming.at[:, own_cols],
                 send_sem.at[k],
                 recv_sem.at[row],
                 pre,
@@ -124,28 +134,30 @@
             )
         )
         copies[-1].start()
-    load.wait()
     mine = row // per_student
-
-    def project(k, total):
-        source = (row - k + row_count) % row_count
-        remote(
-            outgoing.at[0], incoming.at[source], send_sem.at[0], recv_sem.at[source], pre, row
-        ).wait_recv()
-        block = hidden[:, pl.ds(pl.multiple_of(source * depth, depth), depth)]
-        return total + dot(incoming[source], block, 1, 1)
-
-    own = dot(outgoing[mine], hidden[:, pl.ds(pl.multiple_of(row * depth, depth), depth)], 1, 1)
-    total = lax.fori_loop(1, row_count, project, own)
-    latent = total.astype(BF16)
-    latent_ref[...] = latent
+    incoming[:, own_cols] = outgoing[mine]
     place = lax.broadcasted_iota(jnp.int32, (RANK, ranks), 0)
     column = lax.broadcasted_iota(jnp.int32, (RANK, ranks), 1)
     own_pick = jnp.where(column == ids_ref[mine] * RANK + place, 1.0, 0.0).astype(BF16)
-    up = dot(own_pick, up_ref[...], 1, 0).astype(BF16)
+    for copy in loads[1:]:
+        copy.wait()
+    up = dot(own_pick, up_rows[...], 1, 0).astype(BF16)
     own_up_ref[...] = up
+
+    def take(k, carry):
+        source = (row + k) % row_count
+        cols = pl.ds(pl.multiple_of(source * depth, depth), depth)
+        remote(
+            outgoing.at[0], incoming.at[:, cols], send_sem.at[0], recv_sem.at[source], pre, row
+        ).wait_recv()
+        return carry
+
+    lax.fori_loop(1, row_count, take, 0)
+    total = dot(incoming[...], hidden[...], 1, 1)
+    latent = total.astype(BF16)
+    latent_ref[...] = latent
     raised = dot(latent, up, 0, 0)
-    query_ref[...] = (base_ref[...].astype(F32) + ADAPTER_SCALE * raised).astype(BF16)
+    query_ref[...] = (base_rows[...].astype(F32) + ADAPTER_SCALE * raised).astype(BF16)
 
     for copy in copies:
         copy.wait_send()
@@ -165,10 +177,10 @@
     row_count,
     per_student,
     mask_ref,
-    query_ref,
-    upstream_ref,
-    key_ref,
-    value_ref,
+    query_hbm,
+    upstream_hbm,
+    key_hbm,
+    value_hbm,
     latent_ref,
     up_ref,
     hidden_hbm,
@@ -183,7 +195,9 @@
     weights,
     high_rows,
     delta_rows,
-    local,
+    sum_rows,
+    both_rows,
+    back_rows,
     part,
     stat,
     stat_out,
@@ -203,6 +217,7 @@
     up_in,
     raised,
     load_sem,
+    input_sem,
     stat_send,
     stat_recv,
     chain_send,
@@ -222,9 +237,9 @@
 ):
     pre = lax.axis_index("pre")
     row = lax.axis_index("row")
-    tokens = query_ref.shape[0]
-    heads = query_ref.shape[1] // HD
-    keys = key_ref.shape[0]
+    tokens = query_hbm.shape[0]
+    heads = query_hbm.shape[1] // HD
+    keys = key_hbm.shape[0]
     own_rows = heads * tokens // pre_count
     pieces = tokens // own_rows
     half = pre_count // 2
@@ -240,6 +255,23 @@
     line = line_offsets(pre_count)
     barrier = pltpu.get_barrier_semaphore()
 
+    loads = [
+        pltpu.make_async_copy(key_hbm, value_key.at[:, HD:], input_sem.at[0]),
+        pltpu.make_async_copy(value_hbm, value_key.at[:, :HD], input_sem.at[1]),
+    ]
+    for n, (source, landing) in enumerate(((query_hbm, q_rows), (upstream_hbm, u_rows))):
+        for h in range(heads):
+            loads.append(
+                pltpu.make_async_copy(
+                    source.at[:, h * HD : (h + 1) * HD],
+                    landing.at[h * tokens : (h + 1) * tokens, :],
+                    input_sem.at[2 + n * heads + h],
+                )
+            )
+    for copy in loads:
+        copy.start()
+    load = pltpu.make_async_copy(hidden_hbm, hidden, load_sem)
+    load.start()
     for k in line:
         pl.semaphore_signal(
             barrier, inc=1, device_id=((pre + k) % pre_count, row), device_id_type=MESH
@@ -248,60 +280,59 @@
         pl.semaphore_signal(
             barrier, inc=1, device_id=(pre, plane_peer(row, extent, offset)), device_id_type=MESH
         )
-    load = pltpu.make_async_copy(hidden_hbm, hidden, load_sem)
-    load.start()
-
-    value_key[:, :HD] = value_ref[...]
-    value_key[:, HD:] = key_ref[...]
-    for h in range(heads):
-        q_rows[h * tokens : (h + 1) * tokens, :] = query_ref[:, h * HD : (h + 1) * HD]
-        u_rows[h * tokens : (h + 1) * tokens, :] = upstream_ref[:, h * HD : (h + 1) * HD]
+
     for b in range(keys // MB):
         read = jnp.full((8, MB), mask_ref[student, b], jnp.int32)
         bias[:, b * MB : (b + 1) * MB] = jnp.where(read > 0, 0.0, DEAD)
-    block = min(BLOCK, heads * tokens)
-    step = min(512, keys)
+    rows_all = heads * tokens
+    step = weights.shape[2]
     lane = lax.broadcasted_iota(jnp.int32, (tokens, HD), 1)
-    stat[...] = jnp.zeros((tokens, HD), F32)
-
-    def forward(i, carry):
-        rows = pl.ds(pl.multiple_of(i * block, block), block)
-        q = q_rows[rows, :]
-        high = jnp.full((block, HD), FLOOR, F32)
-        for j in range(keys // step):
-            cols = slice(j * step, (j + 1) * step)
-            s = dot(q, key_ref[cols, :], 1, 1) + bias[0:1, cols]
-            weights[rows, cols] = s
-            for g in range(step // HD):
-                high = jnp.maximum(high, s[:, g * HD : (g + 1) * HD])
-        m = jnp.max(high, axis=1, keepdims=True)
-        sums = jnp.zeros((block, HD), F32)
-        both = jnp.zeros((block, 2 * HD), F32)
-        for j in range(keys // step):
-            cols = slice(j * step, (j + 1) * step)
-            w = jnp.exp2((weights[rows, cols] - m) * fold)
-            weights[rows, cols] = w
-            for g in range(step // HD):
-                sums = sums + w[:, g * HD : (g + 1) * HD]
-            both = both + dot(w.astype(BF16), value_key[cols, :], 1, 0)
-        l = jnp.maximum(jnp.sum(sums, axis=1, keepdims=True), TINY)
-        o = both[:, :HD]
-        d = jnp.sum(u_rows[rows, :].astype(F32) * o, axis=1, keepdims=True) / l
-        lse = m * fold + jnp.log(l) * LOG2E
-        high_rows[rows, :] = jnp.broadcast_to(m * fold, (block, HD))
-        delta_rows[rows, :] = jnp.broadcast_to(d, (block, HD))
-        local[0, rows, :] = o
-        local[1, rows, :] = both[:, HD:]
-        table = stat[...]
-        for n in range(block // tokens):
-            h = i * (block // tokens) + n
-            piece_rows = slice(n * tokens, (n + 1) * tokens)
-            table = jnp.where(lane == h, lse[piece_rows], table)
-            table = jnp.where(lane == heads + h, d[piece_rows], table)
-        stat[...] = table
+    high_rows[...] = jnp.full((rows_all, HD), FLOOR, F32)
+    for copy in loads:
+        copy.wait()
+
+    def score(j, carry):
+        cols = pl.ds(pl.multiple_of(j * step, step), step)
+        s = dot(q_rows[...], value_key[cols, HD:], 1, 1) + bias[0:1, cols]
+        weights[j] = s
+        high = high_rows[...]
+        for g in range(step // HD):
+            high = jnp.maximum(high, s[:, g * HD : (g + 1) * HD])
+        high_rows[...] = high
         return carry
 
-    lax.fori_loop(0, heads * tokens // block, forward, 0)
+    lax.fori_loop(0, keys // step, score, 0)
+    top = jnp.max(high_rows[...], axis=1, keepdims=True) * fold
+    high_rows[...] = jnp.broadcast_to(top, (rows_all, HD))
+    sum_rows[...] = jnp.zeros((rows_all, HD), F32)
+    both_rows[...] = jnp.zeros((rows_all, 2 * HD), F32)
+
+    def weigh(j, carry):
+        cols = pl.ds(pl.multiple_of(j * step, step), step)
+        level = high_rows[...]
+        sums = sum_rows[...]
+        ws = []
+        for g in range(step // HD):
+            w = jnp.exp2(weights[j, :, g * HD : (g + 1) * HD] * fold - level)
+            weights[j, :, g * HD : (g + 1) * HD] = w
+            sums = sums + w
+            ws.append(w.astype(BF16))
+        sum_rows[...] = sums
+        both_rows[...] += dot(jnp.concatenate(ws, axis=1), value_key[cols, :], 1, 0)
+        return carry
+
+    lax.fori_loop(0, keys // step, weigh, 0)
+    table = jnp.zeros((tokens, HD), F32)
+    for h in range(heads):
+        rows = slice(h * tokens, (h + 1) * tokens)
+        l = jnp.maximum(jnp.sum(sum_rows[rows, :], axis=1, keepdims=True), TINY)
+        weighed = u_rows[rows, :].astype(F32) * both_rows[rows, :HD]
+        d = jnp.sum(weighed, axis=1, keepdims=True) / l
+        lse = high_rows[rows, :] + jnp.log(l) * LOG2E
+        delta_rows[rows, :] = jnp.broadcast_to(d, (tokens, HD))
+        table = jnp.where(lane == h, lse, table)
+        table = jnp.where(lane == heads + h, d, table)
+    stat[...] = table
 
     stat_out[...] = stat[...].T[: 2 * heads]
     stat_in[pre] = stat_out[...]
@@ -331,24 +362,20 @@
     for copy in stat_copies:
         copy.start()
 
-    def backward(i, carry):
-        rows = pl.ds(pl.multiple_of(i * block, block), block)
-        u = u_rows[rows, :]
-        d = delta_rows[rows, :]
-        a = jnp.zeros((block, HD), F32)
-        for j in range(keys // step):
-            cols = slice(j * step, (j + 1) * step)
-            dp = dot(u, value_ref[cols, :], 1, 1)
-            w = weights[rows, cols]
-            g = [
-                (w[:, n * HD : (n + 1) * HD] * (dp[:, n * HD : (n + 1) * HD] - d)).astype(BF16)
-                for n in range(step // HD)
-            ]
-            a = a + dot(jnp.concatenate(g, axis=1), key_ref[cols, :], 1, 0)
-        local[2, rows, :] = a
+    back_rows[...] = jnp.zeros((rows_all, HD), F32)
+
+    def backward(j, carry):
+        cols = pl.ds(pl.multiple_of(j * step, step), step)
+        dp = dot(u_rows[...], value_key[cols, :HD], 1, 1)
+        d = delta_rows[...]
+        g = [
+            (weights[j, :, n * HD : (n + 1) * HD] * (dp[:, n * HD : (n + 1) * HD] - d)).astype(BF16)
+            for n in range(step // HD)
+        ]
+        back_rows[...] += dot(jnp.concatenate(g, axis=1), value_key[cols, HD:], 1, 0)
         return carry
 
-    lax.fori_loop(0, heads * tokens // block, backward, 0)
+    lax.fori_loop(0, keys // step, backward, 0)
 
     take_line(stat_out, stat_in, stat_send, stat_recv)
     top = stat_in[0, :heads]
@@ -367,8 +394,8 @@
         rows = slice(h * tokens, (h + 1) * tokens)
         factor = jnp.exp2(high_rows[rows, :] - table[:, h : h + 1])
         shift = delta_rows[rows, :] - table[:, heads + h : heads + h + 1]
-        part[0, rows, :] = (local[2, rows, :] + shift * local[1, rows, :]) * (factor * score_scale)
-        part[1, rows, :] = local[0, rows, :] * factor
+        part[0, rows, :] = (back_rows[rows, :] + shift * both_rows[rows, HD:]) * (factor * score_scale)
+        part[1, rows, :] = both_rows[rows, :HD] * factor
 
     def own_part(which, flow, distance):
         chunk = (pre + (distance if flow == 0 else pre_count - distance)) % pre_count
@@ -398,53 +425,64 @@
         )
 
     sent = []
-    for t in range(steps):
-        for which in (0, 1):
-            if t == 0:
-                chain_out[1, 0, which] = own_part(which, 1, half).astype(BF16)
-                sent.append(chain_copy(1, 0, which))
-                sent[-1].start()
+
+    def start_sums(which):
+        chain_out[1, 0, which] = own_part(which, 1, half).astype(BF16)
+        sent.append(chain_copy(1, 0, which))
+        sent[-1].start()
+        for t in range(steps):
             for flow in (0, 1):
                 odd_out[flow, t, which] = own_part(which, flow, half - 1 - 2 * t).astype(BF16)
                 sent.append(odd_copy(flow, t, which))
                 sent[-1].start()
+
+    def arrivals(flow, t, which, total):
+        odd_copy(flow, t, which).wait_recv()
+        total = total + odd_in[flow, t, which].astype(F32)
+        if flow == 1 or t > 0:
+            chain_copy(flow, t, which).wait_recv()
+            total = total + chain_in[flow, t, which].astype(F32)
+        return total
+
+    def relay(t, which):
+        for flow in (1, 0):
+            total = arrivals(flow, t - 1, which, own_part(which, flow, half - 2 * t))
+            chain_out[flow, t, which] = total.astype(BF16)
+            sent.append(chain_copy(flow, t, which))
+            sent[-1].start()
+
+    def own_sum(which):
+        total = own_part(which, 0, 0)
+        for flow in (0, 1):
+            total = arrivals(flow, steps - 1, which, total)
+        return total.astype(BF16)
+
+    start_sums(0)
     for t in range(1, steps):
-        for which in (0, 1):
-            for flow in (0, 1):
-                total = own_part(which, flow, half - 2 * t)
-                odd_copy(flow, t - 1, which).wait_recv()
-                total = total + odd_in[flow, t - 1, which].astype(F32)
-                if flow == 1 or t > 1:
-                    chain_copy(flow, t - 1, which).wait_recv()
-                    total = total + chain_in[flow, t - 1, which].astype(F32)
-                chain_out[flow, t, which] = total.astype(BF16)
-                sent.append(chain_copy(flow, t, which))
-                sent[-1].start()
+        relay(t, 0)
+        if t == 1:
+            start_sums(1)
+        else:
+            relay(t - 1, 1)
+    if steps == 1:
+        start_sums(1)
 
     head = pre // pieces
     piece = pre % pieces
-    results = []
-    for which in (0, 1):
-        total = own_part(which, 0, 0)
-        for flow in (0, 1):
-            odd_copy(flow, steps - 1, which).wait_recv()
-            total = total + odd_in[flow, steps - 1, which].astype(F32)
-            if flow == 1 or steps > 1:
-                chain_copy(flow, steps - 1, which).wait_recv()
-                total = total + chain_in[flow, steps - 1, which].astype(F32)
-        results.append(total.astype(BF16))
-        if which == 0:
-            grad_q = jnp.concatenate([results[0]] * pieces, axis=0)
-            piece_of = lax.broadcasted_iota(jnp.int32, (tokens, HD), 0) // own_rows
-            grad_q = jnp.where(piece_of == piece, grad_q.astype(F32), 0.0).astype(BF16)
-            up_head = up_ref[:, pl.ds(pl.multiple_of(head * HD, HD), HD)]
-            term_out[:RANK, :] = (ADAPTER_SCALE * dot(up_head, grad_q, 1, 1)).astype(BF16)
-            term_out[RANK:, :] = (ADAPTER_SCALE * dot(latent_ref[...], grad_q, 1, 0)).astype(BF16)
-            term_copies = line_copies(term_out, term_in, term_send, term_recv)
-            for copy in term_copies:
-                copy.start()
-            term_in[pre] = term_out[...]
-    att_in[pre] = results[1]
+    own = own_sum(0)
+    grad_q = jnp.concatenate([own] * pieces, axis=0)
+    piece_of = lax.broadcasted_iota(jnp.int32, (tokens, HD), 0) // own_rows
+    grad_q = jnp.where(piece_of == piece, grad_q.astype(F32), 0.0).astype(BF16)
+    up_head = up_ref[:, pl.ds(pl.multiple_of(head * HD, HD), HD)]
+    term_out[:RANK, :] = (ADAPTER_SCALE * dot(up_head, grad_q, 1, 1)).astype(BF16)
+    term_out[RANK:, :] = (ADAPTER_SCALE * dot(latent_ref[...], grad_q, 1, 0)).astype(BF16)
+    term_copies = line_copies(term_out, term_in, term_send, term_recv)
+    for copy in term_copies:
+        copy.start()
+    term_in[pre] = term_out[...]
+    if steps > 1:
+        relay(steps - 1, 1)
+    att_in[pre] = own_sum(1)
 
     stride = max(pre_count // 4, 1)
     far = [k for k in (2 * stride, stride, 3 * stride) if k < pre_count]
@@ -631,15 +669,18 @@
             jax.ShapeDtypeStruct((tokens, width), BF16),
             jax.ShapeDtypeStruct((RANK, width), BF16),
         ),
-        in_specs=[smem(), vmem(), anywhere(), vmem(), vmem()],
+        in_specs=[smem()] + [anywhere()] * 4,
         out_specs=(vmem(), vmem(), vmem()),
         scratch_shapes=[
             pltpu.VMEM((students, RANK, depth), BF16),
-            pltpu.VMEM((row_count, RANK, depth), BF16),
+            pltpu.VMEM((RANK, model), BF16),
+            pltpu.VMEM((depth, ranks), BF16),
             pltpu.VMEM((tokens, model), BF16),
+            pltpu.VMEM((ranks, width), BF16),
+            pltpu.VMEM((tokens, width), BF16),
             dma((row_count,)),
             dma((row_count,)),
-            dma,
+            dma((4,)),
         ],
         compiler_params=pltpu.CompilerParams(collective_id=0, has_side_effects=True),
         name="queries",
@@ -657,7 +698,7 @@
             jax.ShapeDtypeStruct((row_count, RANK, depth), BF16),
             jax.ShapeDtypeStruct((row_count, RANK, quarter), BF16),
         ),
-        in_specs=[smem()] + [vmem()] * 6 + [anywhere()],
+        in_specs=[smem()] + [anywhere()] * 4 + [vmem()] * 2 + [anywhere()],
         out_specs=(vmem(), vmem(), vmem()),
         scratch_shapes=[
             pltpu.VMEM((tokens, model), BF16),
@@ -665,10 +706,12 @@
             pltpu.VMEM((rows, HD), BF16),
             pltpu.VMEM((8, keys), F32),
             pltpu.VMEM((keys, 2 * HD), BF16),
-            pltpu.VMEM((rows, keys), F32),
+            pltpu.VMEM((keys // STEP, rows, STEP), F32),
             pltpu.VMEM((rows, HD), F32),
             pltpu.VMEM((rows, HD), F32),
-            pltpu.VMEM((3, rows, HD), F32),
+            pltpu.VMEM((rows, HD), F32),
+            pltpu.VMEM((rows, 2 * HD), F32),
+            pltpu.VMEM((rows, HD), F32),
             pltpu.VMEM((2, rows, HD), F32),
             pltpu.VMEM((tokens, HD), F32),
             pltpu.VMEM((2 * heads, tokens), F32),
@@ -688,6 +731,7 @@
             pltpu.VMEM((row_count, RANK, quarter), BF16),
             pltpu.VMEM((RANK, width), F32),
             dma,
+            dma((2 + 2 * heads,)),
             dma((pre_count,)),
             dma((pre_count,)),
             dma(ring),

time: 86.1 us -> 84 us (0.976)
  the two profiles are of different devices: /device:TPU:1 before, /device:TPU:6 now
where the time goes in v3:
time: 84 us; the launch traced here: 83.7 us
  Pallas kernels  83 us (99%)
    pallas_call x1, Pallas kernels, shards(): pl.pallas_call(functools.partial(attention_kernel, pre_count, row_count,...  64.3 us
    pallas_call x1, Pallas kernels, shards(): pl.pallas_call(functools.partial(query_kernel, per_student, row_count), o...  16.4 us
    pallas_call x1, Pallas kernels, shards(): pl.pallas_call(functools.partial(output_kernel, per_student), out_shape=(...  2.33 us

profile of v3, /device:TPU:6, one launch (start us, length us, event | category | flops | bytes accessed | tf_op | source)
XLA Modules:
  0.0 83.7 jit_solution(10026897310974931173)
XLA Ops:
  0.6 16.4 %queries.1 = (bf16[16,128]{1,0:T(8,128)(2,1)}, bf16[128,1024]{1,0:T(8,128)(2,1)}, bf16[16,1024]{1,0:T(8,128)(2,1)}) custom-call(s32[8]{0:T(128)} %ids_ref.3, bf16[256,128]{1,0:T(8,128)(2,1)} %a_hbm.1, bf16[128,8192]{1,0:T(8,128)(2,1)} %hidden_hbm.3, bf16[128,1024]{1,0:T(8,128)(2,1)} %up_hbm.1, bf16[128,1024]{1,0:T(8,128)(2,1)} %base_hbm.1), custom_call_target="tpu_custom_call" | custom-call | tf_op jit(solution)/shard_map/queries/pallas_call | solution.py:665
  17.0 64.3 %attention.1 = (bf16[16,64,128]{2,1,0:T(8,128)(2,1)}, bf16[32,16,256]{2,1,0:T(8,128)(2,1)}, bf16[32,16,256]{2,1,0:T(8,128)(2,1)}) custom-call(s32[8,16]{1,0:T(8,128)} %mask_ref.1, bf16[128,1024]{1,0:T(8,128)(2,1)} %get-tuple-element.9.query_hbm, bf16[128,1024]{1,0:T(8,128)(2,1)} %upstream_hbm.1, bf16[2048,128]{1,0:T(8,128)(2,1)} %key_hbm.1, ...), custom_call_target="tpu_custom_call" | custom-call | tf_op jit(solution)/shard_map/attention/pallas_call | solution.py:694
  81.3 2.3 %outputs.1 = (bf16[128,1024]{1,0:T(8,128)(2,1)}, f32[256,128]{1,0:T(8,128)}, f32[128,1024]{1,0:T(8,128)}) custom-call(s32[8]{0:T(128)} %ids_ref.3, bf16[16,64,128]{2,1,0:T(8,128)(2,1)} %get-tuple-element.12.att_ref, bf16[32,16,256]{2,1,0:T(8,128)(2,1)} %get-tuple-element.13.grad_ref, bf16[32,16,256]{2,1,0:T(8,128)(2,1)} %get-tuple-element.14.raised_ref), custom_call_target="tpu_custom_call" | custom-call | tf_op jit(solution)/shard_map/outputs/pallas_call | solution.py:755

commit v4 on v3

--- a/solution.py
+++ b/solution.py
@@ -211,6 +211,8 @@
     att_in,
     quarter_out,
     quarter_in,
+    lift_out,
+    lift_in,
     grad_out,
     grad_in,
     up_out,
@@ -230,6 +232,8 @@
     att_recv,
     quarter_send,
     quarter_recv,
+    lift_send,
+    lift_recv,
     grad_send,
     grad_recv,
     up_send,
@@ -241,7 +245,6 @@
     heads = query_hbm.shape[1] // HD
     keys = key_hbm.shape[0]
     own_rows = heads * tokens // pre_count
-    pieces = tokens // own_rows
     half = pre_count // 2
     steps = half // 2
     score_scale = 1.0 / math.sqrt(HD)
@@ -393,124 +396,76 @@
     for h in range(heads):
         rows = slice(h * tokens, (h + 1) * tokens)
         factor = jnp.exp2(high_rows[rows, :] - table[:, h : h + 1])
-        shift = delta_rows[rows, :] - table[:, heads + h : heads + h + 1]
-        part[0, rows, :] = (back_rows[rows, :] + shift * both_rows[rows, HD:]) * (factor * score_scale)
-        part[1, rows, :] = both_rows[rows, :HD] * factor
-
-    def own_part(which, flow, distance):
-        chunk = (pre + (distance if flow == 0 else pre_count - distance)) % pre_count
-        return part[which, pl.ds(pl.multiple_of(chunk * own_rows, own_rows), own_rows), :]
+        high_rows[rows, :] = factor
+        part[rows, :] = both_rows[rows, :HD] * factor
 
     def hop(flow, distance):
         return (pre + (distance if flow == 0 else pre_count - distance)) % pre_count
 
-    def chain_copy(flow, t, which):
+    def own_part(flow, distance):
+        chunk = hop(flow, distance)
+        return part[pl.ds(pl.multiple_of(chunk * own_rows, own_rows), own_rows), :]
+
+    def chain_copy(flow, t):
         return remote(
-            chain_out.at[flow, t, which],
-            chain_in.at[flow, t, which],
-            chain_send.at[flow, t, which],
-            chain_recv.at[flow, t, which],
+            chain_out.at[flow, t],
+            chain_in.at[flow, t],
+            chain_send.at[flow, t],
+            chain_recv.at[flow, t],
             hop(flow, 2),
             row,
         )
 
-    def odd_copy(flow, t, which):
+    def odd_copy(flow, t):
         return remote(
-            odd_out.at[flow, t, which],
-            odd_in.at[flow, t, which],
-            odd_send.at[flow, t, which],
-            odd_recv.at[flow, t, which],
+            odd_out.at[flow, t],
+            odd_in.at[flow, t],
+            odd_send.at[flow, t],
+            odd_recv.at[flow, t],
             hop(flow, 1),
             row,
         )
 
     sent = []
 
-    def start_sums(which):
-        chain_out[1, 0, which] = own_part(which, 1, half).astype(BF16)
-        sent.append(chain_copy(1, 0, which))
-        sent[-1].start()
-        for t in range(steps):
-            for flow in (0, 1):
-                odd_out[flow, t, which] = own_part(which, flow, half - 1 - 2 * t).astype(BF16)
-                sent.append(odd_copy(flow, t, which))
-                sent[-1].start()
-
-    def arrivals(flow, t, which, total):
-        odd_copy(flow, t, which).wait_recv()
-        total = total + odd_in[flow, t, which].astype(F32)
+    def arrivals(flow, t, total):
+        odd_copy(flow, t).wait_recv()
+        total = total + odd_in[flow, t].astype(F32)
         if flow == 1 or t > 0:
-            chain_copy(flow, t, which).wait_recv()
-            total = total + chain_in[flow, t, which].astype(F32)
+            chain_copy(flow, t).wait_recv()
+            total = total + chain_in[flow, t].astype(F32)
         return total
 
-    def relay(t, which):
+    def relay(t):
         for flow in (1, 0):
-            total = arrivals(flow, t - 1, which, own_part(which, flow, half - 2 * t))
-            chain_out[flow, t, which] = total.astype(BF16)
-            sent.append(chain_copy(flow, t, which))
+            total = arrivals(flow, t - 1, own_part(flow, half - 2 * t))
+            chain_out[flow, t] = total.astype(BF16)
+            sent.append(chain_copy(flow, t))
             sent[-1].start()
 
-    def own_sum(which):
-        total = own_part(which, 0, 0)
+    chain_out[1, 0] = own_part(1, half).astype(BF16)
+    sent.append(chain_copy(1, 0))
+    sent[-1].start()
+    for t in range(steps):
         for flow in (0, 1):
-            total = arrivals(flow, steps - 1, which, total)
-        return total.astype(BF16)
-
-    start_sums(0)
-    for t in range(1, steps):
-        relay(t, 0)
-        if t == 1:
-            start_sums(1)
-        else:
-            relay(t - 1, 1)
-    if steps == 1:
-        start_sums(1)
-
-    head = pre // pieces
-    piece = pre % pieces
-    own = own_sum(0)
-    grad_q = jnp.concatenate([own] * pieces, axis=0)
-    piece_of = lax.broadcasted_iota(jnp.int32, (tokens, HD), 0) // own_rows
-    grad_q = jnp.where(piece_of == piece, grad_q.astype(F32), 0.0).astype(BF16)
-    up_head = up_ref[:, pl.ds(pl.multiple_of(head * HD, HD), HD)]
-    term_out[:RANK, :] = (ADAPTER_SCALE * dot(up_head, grad_q, 1, 1)).astype(BF16)
-    term_out[RANK:, :] = (ADAPTER_SCALE * dot(latent_ref[...], grad_q, 1, 0)).astype(BF16)
+            odd_out[flow, t] = own_part(flow, half - 1 - 2 * t).astype(BF16)
+            sent.append(odd_copy(flow, t))
+            sent[-1].start()
+
+    code = jnp.zeros((RANK, tokens), F32)
+    for h in range(heads):
+        rows = slice(h * tokens, (h + 1) * tokens)
+        cols = slice(h * HD, (h + 1) * HD)
+        shift = delta_rows[rows, :] - table[:, heads + h : heads + h + 1]
+        grad_q = (back_rows[rows, :] + shift * both_rows[rows, HD:]) * (high_rows[rows, :] * score_scale)
+        grad_q = grad_q.astype(BF16)
+        code = code + dot(up_ref[:, cols], grad_q, 1, 1)
+        raised[:, cols] = ADAPTER_SCALE * dot(latent_ref[...], grad_q, 1, 0)
+    term_out[...] = (ADAPTER_SCALE * code).astype(BF16)
     term_copies = line_copies(term_out, term_in, term_send, term_recv)
     for copy in term_copies:
         copy.start()
     term_in[pre] = term_out[...]
-    if steps > 1:
-        relay(steps - 1, 1)
-    att_in[pre] = own_sum(1)
-
-    stride = max(pre_count // 4, 1)
-    far = [k for k in (2 * stride, stride, 3 * stride) if k < pre_count]
-    near = [k if k <= stride // 2 else k - stride for k in range(1, stride)]
-
-    def att_copy(slot, n, k):
-        return remote(
-            att_in.at[slot],
-            att_in.at[slot],
-            att_send.at[n],
-            att_recv.at[slot],
-            (pre + k + pre_count) % pre_count,
-            row,
-        )
-
-    att_copies = [att_copy(pre, n, k) for n, k in enumerate(far)]
-    for copy in att_copies:
-        copy.start()
-
-    load.wait()
-    take_line(term_out, term_in, term_send, term_recv)
-    code = jnp.zeros((RANK, tokens), F32)
-    for h in range(heads):
-        lifted = jnp.zeros((RANK, HD), F32)
-        for n in range(pieces):
-            code = code + term_in[h * pieces + n, :RANK, :].astype(F32)
-            lifted = lifted + term_in[h * pieces + n, RANK:, :].astype(F32)
-        raised[:, h * HD : (h + 1) * HD] = lifted
     for n in range(per_student):
         quarter_out[n] = raised[:, n * width : (n + 1) * width].astype(BF16)
 
@@ -528,19 +483,8 @@
     for k in range(1, per_student):
         quarter_copy(k).start()
     quarter_in[place] = quarter_out[place]
-    code = code.astype(BF16)
-
-    grad_copies = []
-    for n, offset in enumerate(plane):
-        to = plane_peer(row, extent, offset)
-        cols = pl.ds(pl.multiple_of(to * depth, depth), depth)
-        grad_out[to] = dot(code, hidden[:, cols], 1, 0).astype(BF16)
-        grad_copies.append(
-            remote(grad_out.at[to], grad_in.at[row], grad_send.at[n], grad_recv.at[row], pre, to)
-        )
-        grad_copies[-1].start()
-    cols = pl.ds(pl.multiple_of(row * depth, depth), depth)
-    grad_in[row] = dot(code, hidden[:, cols], 1, 0).astype(BF16)
+    if steps > 1:
+        relay(1)
 
     for k in range(1, per_student):
         origin = (place + k) % per_student
@@ -555,6 +499,61 @@
     summed = jnp.zeros((RANK, width), F32)
     for n in range(per_student):
         summed = summed + quarter_in[n].astype(F32)
+    lift_out[...] = summed.astype(BF16)
+    lift_copies = line_copies(lift_out, lift_in, lift_send, lift_recv)
+    for copy in lift_copies:
+        copy.start()
+    lift_in[pre] = lift_out[...]
+    if steps > 2:
+        relay(2)
+
+    load.wait()
+    take_line(term_out, term_in, term_send, term_recv)
+    code = term_in[0].astype(F32)
+    for n in range(1, pre_count):
+        code = code + term_in[n].astype(F32)
+    code = code.astype(BF16)
+    grad_copies = []
+    for n, offset in enumerate(plane):
+        to = plane_peer(row, extent, offset)
+        cols = pl.ds(pl.multiple_of(to * depth, depth), depth)
+        grad_out[to] = dot(code, hidden[:, cols], 1, 0).astype(BF16)
+        grad_copies.append(
+            remote(grad_out.at[to], grad_in.at[row], grad_send.at[n], grad_recv.at[row], pre, to)
+        )
+        grad_copies[-1].start()
+    cols = pl.ds(pl.multiple_of(row * depth, depth), depth)
+    grad_in[row] = dot(code, hidden[:, cols], 1, 0).astype(BF16)
+    for t in range(3, steps):
+        relay(t)
+
+    total = own_part(0, 0)
+    for flow in (0, 1):
+        total = arrivals(flow, steps - 1, total)
+    att_in[pre] = total.astype(BF16)
+
+    stride = max(pre_count // 4, 1)
+    far = [k for k in (2 * stride, stride, 3 * stride) if k < pre_count]
+    near = [k if k <= stride // 2 else k - stride for k in range(1, stride)]
+
+    def att_copy(slot, n, k):
+        return remote(
+            att_in.at[slot],
+            att_in.at[slot],
+            att_send.at[n],
+            att_recv.at[slot],
+            (pre + k + pre_count) % pre_count,
+            row,
+        )
+
+    att_copies = [att_copy(pre, n, k) for n, k in enumerate(far)]
+    for copy in att_copies:
+        copy.start()
+
+    take_line(lift_out, lift_in, lift_send, lift_recv)
+    summed = lift_in[0].astype(F32)
+    for n in range(1, pre_count):
+        summed = summed + lift_in[n].astype(F32)
     up_out[...] = summed.astype(BF16)
     up_copies = []
     for n, offset in enumerate(plane):
@@ -597,7 +596,7 @@
     lax.fori_loop(1, row_count, take_up, 0)
     raised_ref[...] = up_in[...]
 
-    for copy in stat_copies + sent + term_copies + att_copies + grad_copies + up_copies:
+    for copy in stat_copies + sent + term_copies + lift_copies + att_copies + grad_copies + up_copies:
         copy.wait_send()
     for k in range(1, per_student):
         quarter_copy(k).wait_send()
@@ -690,7 +689,7 @@
     own_rows = rows // pre_count
     steps = pre_count // 4
     quarter = width // per_student
-    ring = (2, steps, 2)
+    ring = (2, steps)
     att, grad, raised = pl.pallas_call(
         functools.partial(attention_kernel, pre_count, row_count, per_student),
         out_shape=(
@@ -712,7 +711,7 @@
             pltpu.VMEM((rows, HD), F32),
             pltpu.VMEM((rows, 2 * HD), F32),
             pltpu.VMEM((rows, HD), F32),
-            pltpu.VMEM((2, rows, HD), F32),
+            pltpu.VMEM((rows, HD), F32),
             pltpu.VMEM((tokens, HD), F32),
             pltpu.VMEM((2 * heads, tokens), F32),
             pltpu.VMEM((pre_count, 2 * heads, tokens), F32),
@@ -720,11 +719,13 @@
             pltpu.VMEM(ring + (own_rows, HD), BF16),
             pltpu.VMEM(ring + (own_rows, HD), BF16),
             pltpu.VMEM(ring + (own_rows, HD), BF16),
-            pltpu.VMEM((2 * RANK, HD), BF16),
-            pltpu.VMEM((pre_count, 2 * RANK, HD), BF16),
+            pltpu.VMEM((RANK, tokens), BF16),
+            pltpu.VMEM((pre_count, RANK, tokens), BF16),
             pltpu.VMEM((pre_count, own_rows, HD), BF16),
             pltpu.VMEM((per_student, RANK, quarter), BF16),
             pltpu.VMEM((per_student, RANK, quarter), BF16),
+            pltpu.VMEM((RANK, quarter), BF16),
+            pltpu.VMEM((pre_count, RANK, quarter), BF16),
             pltpu.VMEM((row_count, RANK, depth), BF16),
             pltpu.VMEM((row_count, RANK, depth), BF16),
             pltpu.VMEM((RANK, quarter), BF16),
@@ -744,6 +745,8 @@
             dma((pre_count,)),
             dma((per_student,)),
             dma((per_student,)),
+            dma((pre_count,)),
+            dma((pre_count,)),
             dma((row_count,)),
             dma((row_count,)),
             dma((row_count,)),

time: 84 us -> 79.1 us (0.942)
  the two profiles are of different devices: /device:TPU:6 before, /device:TPU:2 now
where the time goes in v4:
time: 79.1 us; the launch traced here: 78.8 us
  Pallas kernels  78.2 us (99%)
    pallas_call x1, Pallas kernels, shards(): pl.pallas_call(functools.partial(attention_kernel, pre_count, row_count,...  59.1 us
    pallas_call x1, Pallas kernels, shards(): pl.pallas_call(functools.partial(query_kernel, per_student, row_count), o...  16.8 us
    pallas_call x1, Pallas kernels, shards(): pl.pallas_call(functools.partial(output_kernel, per_student), out_shape=(...  2.33 us

profile of v4, /device:TPU:2, one launch (start us, length us, event | category | flops | bytes accessed | tf_op | source)
XLA Modules:
  0.0 78.8 jit_solution(1999436604847158996)
XLA Ops:
  0.6 16.8 %queries.1 = (bf16[16,128]{1,0:T(8,128)(2,1)}, bf16[128,1024]{1,0:T(8,128)(2,1)}, bf16[16,1024]{1,0:T(8,128)(2,1)}) custom-call(s32[8]{0:T(128)} %ids_ref.3, bf16[256,128]{1,0:T(8,128)(2,1)} %a_hbm.1, bf16[128,8192]{1,0:T(8,128)(2,1)} %hidden_hbm.3, bf16[128,1024]{1,0:T(8,128)(2,1)} %up_hbm.1, bf16[128,1024]{1,0:T(8,128)(2,1)} %base_hbm.1), custom_call_target="tpu_custom_call" | custom-call | tf_op jit(solution)/shard_map/queries/pallas_call | solution.py:664
  17.4 59.1 %attention.1 = (bf16[16,64,128]{2,1,0:T(8,128)(2,1)}, bf16[32,16,256]{2,1,0:T(8,128)(2,1)}, bf16[32,16,256]{2,1,0:T(8,128)(2,1)}) custom-call(s32[8,16]{1,0:T(8,128)} %mask_ref.1, bf16[128,1024]{1,0:T(8,128)(2,1)} %get-tuple-element.9.query_hbm, bf16[128,1024]{1,0:T(8,128)(2,1)} %upstream_hbm.1, bf16[2048,128]{1,0:T(8,128)(2,1)} %key_hbm.1, ...), custom_call_target="tpu_custom_call" | custom-call | tf_op jit(solution)/shard_map/attention/pallas_call | solution.py:693
  76.5 2.3 %outputs.1 = (bf16[128,1024]{1,0:T(8,128)(2,1)}, f32[256,128]{1,0:T(8,128)}, f32[128,1024]{1,0:T(8,128)}) custom-call(s32[8]{0:T(128)} %ids_ref.3, bf16[16,64,128]{2,1,0:T(8,128)(2,1)} %get-tuple-element.12.att_ref, bf16[32,16,256]{2,1,0:T(8,128)(2,1)} %get-tuple-element.13.grad_ref, bf16[32,16,256]{2,1,0:T(8,128)(2,1)} %get-tuple-element.14.raised_ref), custom_call_target="tpu_custom_call" | custom-call | tf_op jit(solution)/shard_map/outputs/pallas_call | solution.py:758

commit v5 on v4

--- a/solution.py
+++ b/solution.py
@@ -202,10 +202,8 @@
     stat,
     stat_out,
     stat_in,
-    chain_out,
-    chain_in,
-    odd_out,
-    odd_in,
+    sum_out,
+    sum_in,
     term_out,
     term_in,
     att_in,
@@ -222,10 +220,8 @@
     input_sem,
     stat_send,
     stat_recv,
-    chain_send,
-    chain_recv,
-    odd_send,
-    odd_recv,
+    sum_send,
+    sum_recv,
     term_send,
     term_recv,
     att_send,
@@ -246,7 +242,7 @@
     keys = key_hbm.shape[0]
     own_rows = heads * tokens // pre_count
     half = pre_count // 2
-    steps = half // 2
+    stride = half // 2
     score_scale = 1.0 / math.sqrt(HD)
     fold = score_scale * LOG2E
     student = row // per_student
@@ -406,51 +402,39 @@
         chunk = hop(flow, distance)
         return part[pl.ds(pl.multiple_of(chunk * own_rows, own_rows), own_rows), :]
 
-    def chain_copy(flow, t):
+    def sum_copy(flow, distance):
         return remote(
-            chain_out.at[flow, t],
-            chain_in.at[flow, t],
-            chain_send.at[flow, t],
-            chain_recv.at[flow, t],
-            hop(flow, 2),
+            sum_out.at[flow, distance],
+            sum_in.at[flow, distance],
+            sum_send.at[flow, distance],
+            sum_recv.at[flow, distance],
+            hop(flow, distance if distance <= stride else distance - stride),
             row,
         )
 
-    def odd_copy(flow, t):
-        return remote(
-            odd_out.at[flow, t],
-            odd_in.at[flow, t],
-            odd_send.at[flow, t],
-            odd_recv.at[flow, t],
-            hop(flow, 1),
-            row,
-        )
+    def reach(flow):
+        return half - 1 + flow
 
     sent = []
 
-    def arrivals(flow, t, total):
-        odd_copy(flow, t).wait_recv()
-        total = total + odd_in[flow, t].astype(F32)
-        if flow == 1 or t > 0:
-            chain_copy(flow, t).wait_recv()
-            total = total + chain_in[flow, t].astype(F32)
+    def send_sum(flow, distance, total):
+        sum_out[flow, distance] = total.astype(BF16)
+        sent.append(sum_copy(flow, distance))
+        sent[-1].start()
+
+    def arrivals(flow, distances, total):
+        for distance in distances:
+            sum_copy(flow, distance).wait_recv()
+            total = total + sum_in[flow, distance].astype(F32)
         return total
 
-    def relay(t):
+    for distance in range(half, stride, -1):
         for flow in (1, 0):
-            total = arrivals(flow, t - 1, own_part(flow, half - 2 * t))
-            chain_out[flow, t] = total.astype(BF16)
-            sent.append(chain_copy(flow, t))
-            sent[-1].start()
-
-    chain_out[1, 0] = own_part(1, half).astype(BF16)
-    sent.append(chain_copy(1, 0))
-    sent[-1].start()
-    for t in range(steps):
-        for flow in (0, 1):
-            odd_out[flow, t] = own_part(flow, half - 1 - 2 * t).astype(BF16)
-            sent.append(odd_copy(flow, t))
-            sent[-1].start()
+            if distance <= reach(flow):
+                send_sum(flow, distance, own_part(flow, distance))
+    for distance in range(stride - 1, 0, -1):
+        for flow in (1, 0):
+            send_sum(flow, distance, own_part(flow, distance))
 
     code = jnp.zeros((RANK, tokens), F32)
     for h in range(heads):
@@ -483,8 +467,6 @@
     for k in range(1, per_student):
         quarter_copy(k).start()
     quarter_in[place] = quarter_out[place]
-    if steps > 1:
-        relay(1)
 
     for k in range(1, per_student):
         origin = (place + k) % per_student
@@ -504,8 +486,9 @@
     for copy in lift_copies:
         copy.start()
     lift_in[pre] = lift_out[...]
-    if steps > 2:
-        relay(2)
+    for flow in (1, 0):
+        beyond = range(stride + 1, reach(flow) + 1)
+        send_sum(flow, stride, arrivals(flow, beyond, own_part(flow, stride)))
 
     load.wait()
     take_line(term_out, term_in, term_send, term_recv)
@@ -524,31 +507,30 @@
         grad_copies[-1].start()
     cols = pl.ds(pl.multiple_of(row * depth, depth), depth)
     grad_in[row] = dot(code, hidden[:, cols], 1, 0).astype(BF16)
-    for t in range(3, steps):
-        relay(t)
 
     total = own_part(0, 0)
     for flow in (0, 1):
-        total = arrivals(flow, steps - 1, total)
+        total = arrivals(flow, range(1, stride + 1), total)
     att_in[pre] = total.astype(BF16)
-
-    stride = max(pre_count // 4, 1)
-    far = [k for k in (2 * stride, stride, 3 * stride) if k < pre_count]
-    near = [k if k <= stride // 2 else k - stride for k in range(1, stride)]
-
-    def att_copy(slot, n, k):
-        return remote(
-            att_in.at[slot],
-            att_in.at[slot],
-            att_send.at[n],
-            att_recv.at[slot],
-            (pre + k + pre_count) % pre_count,
-            row,
-        )
-
-    att_copies = [att_copy(pre, n, k) for n, k in enumerate(far)]
-    for copy in att_copies:
-        copy.start()
+    att_copies = []
+
+    def give(slot, flow, distance):
+        n = len(att_copies)
+        att_copies.append(
+            remote(
+                att_in.at[slot],
+                att_in.at[slot],
+                att_send.at[n],
+                att_recv.at[slot],
+                hop(flow, distance),
+                row,
+            )
+        )
+        att_copies[-1].start()
+
+    for distance in range(stride, 0, -1):
+        for flow in (1, 0):
+            give(pre, flow, distance)
 
     take_line(lift_out, lift_in, lift_send, lift_recv)
     summed = lift_in[0].astype(F32)
@@ -569,13 +551,11 @@
             landing.at[slot], landing.at[slot], send_sem.at[0], recv_sem.at[slot], pre, row
         ).wait_recv()
 
-    for k in far:
-        slot_wait(att_in, (pre + k) % pre_count, att_send, att_recv)
-    for k in near:
-        for n in range(len(far) + 1):
-            slot = (pre + n * stride) % pre_count
-            att_copies.append(att_copy(slot, len(att_copies), k))
-            att_copies[-1].start()
+    for flow in (1, 0):
+        behind = hop(1 - flow, stride)
+        slot_wait(att_in, behind, att_send, att_recv)
+        for distance in range(reach(flow) - stride, 0, -1):
+            give(behind, flow, distance)
 
     def take_grad(k, carry):
         slot_wait(grad_in, (row + k) % row_count, grad_send, grad_recv)
@@ -583,10 +563,9 @@
 
     lax.fori_loop(1, row_count, take_grad, 0)
     grad_ref[...] = grad_in[...]
-    for k in near:
-        for n in range(len(far) + 1):
-            slot = (pre - k + n * stride + pre_count) % pre_count
-            slot_wait(att_in, slot, att_send, att_recv)
+    for k in range(1, pre_count):
+        if k not in (stride, pre_count - stride):
+            slot_wait(att_in, (pre + k) % pre_count, att_send, att_recv)
     attended_ref[...] = att_in[...]
 
     def take_up(k, carry):
@@ -687,9 +666,8 @@
 
     rows = heads * tokens
     own_rows = rows // pre_count
-    steps = pre_count // 4
     quarter = width // per_student
-    ring = (2, steps)
+    ring = (2, pre_count // 2 + 1)
     att, grad, raised = pl.pallas_call(
         functools.partial(attention_kernel, pre_count, row_count, per_student),
         out_shape=(
@@ -717,8 +695,6 @@
             pltpu.VMEM((pre_count, 2 * heads, tokens), F32),
             pltpu.VMEM(ring + (own_rows, HD), BF16),
             pltpu.VMEM(ring + (own_rows, HD), BF16),
-            pltpu.VMEM(ring + (own_rows, HD), BF16),
-            pltpu.VMEM(ring + (own_rows, HD), BF16),
             pltpu.VMEM((RANK, tokens), BF16),
             pltpu.VMEM((pre_count, RANK, tokens), BF16),
             pltpu.VMEM((pre_count, own_rows, HD), BF16),
@@ -735,8 +711,6 @@
             dma((2 + 2 * heads,)),
             dma((pre_count,)),
             dma((pre_count,)),
-            dma(ring),
-            dma(ring),
             dma(ring),
             dma(ring),
             dma((pre_count,)),

time: 79.1 us -> 77.1 us (0.975)
  the two profiles are of different devices: /device:TPU:2 before, /device:TPU:32 now
where the time goes in v5:
time: 77.1 us; the launch traced here: 76.8 us
  Pallas kernels  76.2 us (99%)
    pallas_call x1, Pallas kernels, shards(): pl.pallas_call(functools.partial(attention_kernel, pre_count, row_count,...  58.8 us
    pallas_call x1, Pallas kernels, shards(): pl.pallas_call(functools.partial(query_kernel, per_student, row_count), o...  15 us
    pallas_call x1, Pallas kernels, shards(): pl.pallas_call(functools.partial(output_kernel, per_student), out_shape=(...  2.33 us

profile of v5, /device:TPU:32, one launch (start us, length us, event | category | flops | bytes accessed | tf_op | source)
XLA Modules:
  0.0 76.8 jit_solution(7527072741825304947)
XLA Ops:
  0.6 15.0 %queries.1 = (bf16[16,128]{1,0:T(8,128)(2,1)}, bf16[128,1024]{1,0:T(8,128)(2,1)}, bf16[16,1024]{1,0:T(8,128)(2,1)}) custom-call(s32[8]{0:T(128)} %ids_ref.3, bf16[256,128]{1,0:T(8,128)(2,1)} %a_hbm.1, bf16[128,8192]{1,0:T(8,128)(2,1)} %hidden_hbm.3, bf16[128,1024]{1,0:T(8,128)(2,1)} %up_hbm.1, bf16[128,1024]{1,0:T(8,128)(2,1)} %base_hbm.1), custom_call_target="tpu_custom_call" | custom-call | tf_op jit(solution)/shard_map/queries/pallas_call | solution.py:643
  15.7 58.8 %attention.1 = (bf16[16,64,128]{2,1,0:T(8,128)(2,1)}, bf16[32,16,256]{2,1,0:T(8,128)(2,1)}, bf16[32,16,256]{2,1,0:T(8,128)(2,1)}) custom-call(s32[8,16]{1,0:T(8,128)} %mask_ref.1, bf16[128,1024]{1,0:T(8,128)(2,1)} %get-tuple-element.9.query_hbm, bf16[128,1024]{1,0:T(8,128)(2,1)} %upstream_hbm.1, bf16[2048,128]{1,0:T(8,128)(2,1)} %key_hbm.1, ...), custom_call_target="tpu_custom_call" | custom-call | tf_op jit(solution)/shard_map/attention/pallas_call | solution.py:671
  74.5 2.3 %outputs.1 = (bf16[128,1024]{1,0:T(8,128)(2,1)}, f32[256,128]{1,0:T(8,128)}, f32[128,1024]{1,0:T(8,128)}) custom-call(s32[8]{0:T(128)} %ids_ref.3, bf16[16,64,128]{2,1,0:T(8,128)(2,1)} %get-tuple-element.12.att_ref, bf16[32,16,256]{2,1,0:T(8,128)(2,1)} %get-tuple-element.13.grad_ref, bf16[32,16,256]{2,1,0:T(8,128)(2,1)} %get-tuple-element.14.raised_ref), custom_call_target="tpu_custom_call" | custom-call | tf_op jit(solution)/shard_map/outputs/pallas_call | solution.py:732

commit v6 on v5

--- a/solution.py
+++ b/solution.py
@@ -482,13 +482,37 @@
     for n in range(per_student):
         summed = summed + quarter_in[n].astype(F32)
     lift_out[...] = summed.astype(BF16)
+    for flow in (1, 0):
+        beyond = range(stride + 1, reach(flow) + 1)
+        send_sum(flow, stride, arrivals(flow, beyond, own_part(flow, stride)))
     lift_copies = line_copies(lift_out, lift_in, lift_send, lift_recv)
     for copy in lift_copies:
         copy.start()
     lift_in[pre] = lift_out[...]
-    for flow in (1, 0):
-        beyond = range(stride + 1, reach(flow) + 1)
-        send_sum(flow, stride, arrivals(flow, beyond, own_part(flow, stride)))
+
+    total = own_part(0, 0)
+    for flow in (0, 1):
+        total = arrivals(flow, range(1, stride + 1), total)
+    att_in[pre] = total.astype(BF16)
+    att_copies = []
+
+    def give(slot, flow, distance):
+        n = len(att_copies)
+        att_copies.append(
+            remote(
+                att_in.at[slot],
+                att_in.at[slot],
+                att_send.at[n],
+                att_recv.at[slot],
+                hop(flow, distance),
+                row,
+            )
+        )
+        att_copies[-1].start()
+
+    for distance in range(stride, 0, -1):
+        for flow in (1, 0):
+            give(pre, flow, distance)
 
     load.wait()
     take_line(term_out, term_in, term_send, term_recv)
@@ -507,30 +531,6 @@
         grad_copies[-1].start()
     cols = pl.ds(pl.multiple_of(row * depth, depth), depth)
     grad_in[row] = dot(code, hidden[:, cols], 1, 0).astype(BF16)
-
-    total = own_part(0, 0)
-    for flow in (0, 1):
-        total = arrivals(flow, range(1, stride + 1), total)
-    att_in[pre] = total.astype(BF16)
-    att_copies = []
-
-    def give(slot, flow, distance):
-        n = len(att_copies)
-        att_copies.append(
-            remote(
-                att_in.at[slot],
-                att_in.at[slot],
-                att_send.at[n],
-                att_recv.at[slot],
-                hop(flow, distance),
-                row,
-            )
-        )
-        att_copies[-1].start()
-
-    for distance in range(stride, 0, -1):
-        for flow in (1, 0):
-            give(pre, flow, distance)
 
     take_line(lift_out, lift_in, lift_send, lift_recv)
     summed = lift_in[0].astype(F32)

time: 77.1 us -> 74.2 us (0.962)
  the two profiles are of different devices: /device:TPU:32 before, /device:TPU:1 now
where the time goes in v6:
time: 74.2 us; the launch traced here: 73.9 us
  Pallas kernels  73.3 us (99%)
    pallas_call x1, Pallas kernels, shards(): pl.pallas_call(functools.partial(attention_kernel, pre_count, row_count,...  51.9 us
    pallas_call x1, Pallas kernels, shards(): pl.pallas_call(functools.partial(query_kernel, per_student, row_count), o...  19 us
    pallas_call x1, Pallas kernels, shards(): pl.pallas_call(functools.partial(output_kernel, per_student), out_shape=(...  2.33 us

profile of v6, /device:TPU:1, one launch (start us, length us, event | category | flops | bytes accessed | tf_op | source)
XLA Modules:
  0.0 73.9 jit_solution(2295301201794235796)
XLA Ops:
  0.6 19.0 %queries.1 = (bf16[16,128]{1,0:T(8,128)(2,1)}, bf16[128,1024]{1,0:T(8,128)(2,1)}, bf16[16,1024]{1,0:T(8,128)(2,1)}) custom-call(s32[8]{0:T(128)} %ids_ref.3, bf16[256,128]{1,0:T(8,128)(2,1)} %a_hbm.1, bf16[128,8192]{1,0:T(8,128)(2,1)} %hidden_hbm.3, bf16[128,1024]{1,0:T(8,128)(2,1)} %up_hbm.1, bf16[128,1024]{1,0:T(8,128)(2,1)} %base_hbm.1), custom_call_target="tpu_custom_call" | custom-call | tf_op jit(solution)/shard_map/queries/pallas_call | solution.py:643
  19.7 51.9 %attention.1 = (bf16[16,64,128]{2,1,0:T(8,128)(2,1)}, bf16[32,16,256]{2,1,0:T(8,128)(2,1)}, bf16[32,16,256]{2,1,0:T(8,128)(2,1)}) custom-call(s32[8,16]{1,0:T(8,128)} %mask_ref.1, bf16[128,1024]{1,0:T(8,128)(2,1)} %get-tuple-element.9.query_hbm, bf16[128,1024]{1,0:T(8,128)(2,1)} %upstream_hbm.1, bf16[2048,128]{1,0:T(8,128)(2,1)} %key_hbm.1, ...), custom_call_target="tpu_custom_call" | custom-call | tf_op jit(solution)/shard_map/attention/pallas_call | solution.py:671
  71.6 2.3 %outputs.1 = (bf16[128,1024]{1,0:T(8,128)(2,1)}, f32[256,128]{1,0:T(8,128)}, f32[128,1024]{1,0:T(8,128)}) custom-call(s32[8]{0:T(128)} %ids_ref.3, bf16[16,64,128]{2,1,0:T(8,128)(2,1)} %get-tuple-element.12.att_ref, bf16[32,16,256]{2,1,0:T(8,128)(2,1)} %get-tuple-element.13.grad_ref, bf16[32,16,256]{2,1,0:T(8,128)(2,1)} %get-tuple-element.14.raised_ref), custom_call_target="tpu_custom_call" | custom-call | tf_op jit(solution)/shard_map/outputs/pallas_call | solution.py:732

commit v7 on v6

--- a/solution.py
+++ b/solution.py
@@ -15,7 +15,7 @@
 DEAD = -1e30
 FLOOR = -1e29
 TINY = 1e-30
-STEP = 512
+STEP = 1024
 LOG2E = math.log2(math.e)
 MESH = pl.DeviceIdType.MESH
 F32 = jnp.float32

time: 74.2 us -> 73.8 us (level)
  no operation moved by 1% of the time
where the time goes in v7:
time: 73.8 us; the launch traced here: 73.5 us
  Pallas kernels  72.9 us (99%)
    pallas_call x1, Pallas kernels, shards(): pl.pallas_call(functools.partial(attention_kernel, pre_count, row_count,...  51.5 us
    pallas_call x1, Pallas kernels, shards(): pl.pallas_call(functools.partial(query_kernel, per_student, row_count), o...  19 us
    pallas_call x1, Pallas kernels, shards(): pl.pallas_call(functools.partial(output_kernel, per_student), out_shape=(...  2.33 us

profile of v7, /device:TPU:1, one launch (start us, length us, event | category | flops | bytes accessed | tf_op | source)
XLA Modules:
  0.0 73.5 jit_solution(13372441360955456566)
XLA Ops:
  0.6 19.0 %queries.1 = (bf16[16,128]{1,0:T(8,128)(2,1)}, bf16[128,1024]{1,0:T(8,128)(2,1)}, bf16[16,1024]{1,0:T(8,128)(2,1)}) custom-call(s32[8]{0:T(128)} %ids_ref.3, bf16[256,128]{1,0:T(8,128)(2,1)} %a_hbm.1, bf16[128,8192]{1,0:T(8,128)(2,1)} %hidden_hbm.3, bf16[128,1024]{1,0:T(8,128)(2,1)} %up_hbm.1, bf16[128,1024]{1,0:T(8,128)(2,1)} %base_hbm.1), custom_call_target="tpu_custom_call" | custom-call | tf_op jit(solution)/shard_map/queries/pallas_call | solution.py:643
  19.7 51.5 %attention.1 = (bf16[16,64,128]{2,1,0:T(8,128)(2,1)}, bf16[32,16,256]{2,1,0:T(8,128)(2,1)}, bf16[32,16,256]{2,1,0:T(8,128)(2,1)}) custom-call(s32[8,16]{1,0:T(8,128)} %mask_ref.1, bf16[128,1024]{1,0:T(8,128)(2,1)} %get-tuple-element.9.query_hbm, bf16[128,1024]{1,0:T(8,128)(2,1)} %upstream_hbm.1, bf16[2048,128]{1,0:T(8,128)(2,1)} %key_hbm.1, ...), custom_call_target="tpu_custom_call" | custom-call | tf_op jit(solution)/shard_map/attention/pallas_call | solution.py:671
  71.2 2.3 %outputs.1 = (bf16[128,1024]{1,0:T(8,128)(2,1)}, f32[256,128]{1,0:T(8,128)}, f32[128,1024]{1,0:T(8,128)}) custom-call(s32[8]{0:T(128)} %ids_ref.3, bf16[16,64,128]{2,1,0:T(8,128)(2,1)} %get-tuple-element.12.att_ref, bf16[32,16,256]{2,1,0:T(8,128)(2,1)} %get-tuple-element.13.grad_ref, bf16[32,16,256]{2,1,0:T(8,128)(2,1)} %get-tuple-element.14.raised_ref), custom_call_target="tpu_custom_call" | custom-call | tf_op jit(solution)/shard_map/outputs/pallas_call | solution.py:732
